TPU v7x, 512 devices: a whole 4x8x8 slice. The times are simulated.
512 devices in a mesh: seq: 64 (over y, z), tp: 8 (over x, core).
Axes of the slice: x: 4, y: 8, z: 8, core: 2. Of those that a mesh axis runs over, the one named last changes fastest.
Arguments:
- queries: bfloat16 [49152, 4096], P('seq', 'tp'), may hold values from -6 to 6
- key_rows: bfloat16 [49152, 4096], P('seq', 'tp'), may hold values from -6 to 6
- value_rows: bfloat16 [49152, 4096], P('seq', 'tp'), may hold values from -120 to 120
- log_decay: float32 [32, 49152], P('tp', 'seq'), may hold values from -10 to 0, as said below
- gate_logits: bfloat16 [49152, 4096], P('seq', 'tp'), may hold values from -6 to 6
- norm_gain: float32 [4096], P('tp'), may hold values from 0.1 to 1.9
- out_weight: bfloat16 [4096, 3072], P('tp'), may hold values from -0.125 to 0.125
Outputs:
- projected: bfloat16 [49152, 3072], P('seq', 'tp')
Inputs may be any that keep to these rules, and one draw needn't show every extreme that they name: log_decay is never positive.
All inputs are finite; a program needn't handle non-finite values.
Results may differ from a plain program's by a relative error of at most 0.014.
Values may be sent and summed in bfloat16 or wider, within the bound.
A program may use at most 128 MiB of HBM per device.

v0:
```python
import jax
import jax.numpy as jnp
from jax import lax
from jax.sharding import PartitionSpec as P

HEAD = 128
HEADS = 32
BLOCK = 384


def shards(queries, key_rows, value_rows, log_decay, gate_logits, norm_gain, out_weight):
    rows_here = queries.shape[0]
    columns = queries.shape[1]
    head_count = columns // HEAD
    blocks = rows_here // BLOCK
    query_blocks = queries.reshape(blocks, BLOCK, head_count, HEAD)
    key_blocks = key_rows.reshape(blocks, BLOCK, head_count, HEAD)
    value_blocks = value_rows.reshape(blocks, BLOCK, head_count, HEAD)
    cumulative = jnp.cumsum(log_decay.reshape(head_count, blocks, BLOCK), axis=2)
    totals = cumulative[:, :, -1]
    causal = jnp.tril(jnp.ones((BLOCK, BLOCK), dtype=jnp.bool_))
    spread = cumulative[:, :, :, None] - cumulative[:, :, None, :]
    decays = jnp.where(causal, jnp.exp(jnp.where(causal, spread, 0.0)), 0.0)
    scores = jnp.einsum(
        "ntha,nsha->hnts", query_blocks, key_blocks, preferred_element_type=jnp.float32
    )
    weighted = (scores * decays).astype(jnp.bfloat16)
    inside = jnp.einsum(
        "hnts,nshb->nthb", weighted, value_blocks, preferred_element_type=jnp.float32
    )
    key_scale = jnp.exp(totals[:, :, None] - cumulative).transpose(1, 2, 0)[..., None]
    scaled_keys = (key_blocks.astype(jnp.float32) * key_scale).astype(jnp.bfloat16)
    block_states = jnp.einsum(
        "ntha,nthb->nhab", scaled_keys, value_blocks, preferred_element_type=jnp.float32
    )
    running = jnp.zeros((head_count, HEAD, HEAD), jnp.float32)
    decay_sum = jnp.zeros((head_count,), jnp.float32)
    local_before = []
    decay_before = []
    for block in range(blocks):
        local_before.append(running)
        decay_before.append(decay_sum)
        running = jnp.exp(totals[:, block])[:, None, None] * running + block_states[block]
        decay_sum = decay_sum + totals[:, block]
    all_totals = lax.all_gather(decay_sum[None, :], "seq", axis=0, tiled=True)
    inclusive = jnp.cumsum(all_totals, axis=0)
    position = lax.axis_index("seq")
    before_mine = lax.dynamic_index_in_dim(inclusive - all_totals, position, 0, keepdims=False)
    portion = lax.all_gather(running[None], "seq", axis=0, tiled=True)
    amount = portion.shape[0]
    indices = jnp.arange(amount, dtype=jnp.int32)
    earlier = (indices < position)[:, None]
    factors = jnp.where(
        earlier, jnp.exp(jnp.where(earlier, before_mine[None, :] - inclusive, 0.0)), 0.0
    )
    incoming = jnp.einsum("mh,mhab->hab", factors, portion, precision=lax.Precision.HIGHEST)
    starts = jnp.stack(
        [
            jnp.exp(decay_before[block])[:, None, None] * incoming + local_before[block]
            for block in range(blocks)
        ]
    )
    query_scale = jnp.exp(cumulative).transpose(1, 2, 0)[..., None]
    scaled_queries = query_blocks.astype(jnp.float32) * query_scale
    carried = jnp.einsum("ntha,nhab->nthb", scaled_queries, starts, precision=lax.Precision.HIGHEST)
    attention = (inside + carried).reshape(rows_here, columns)
    squares = lax.psum(jnp.sum(attention * attention, axis=1), "tp")
    mean_square = squares / (HEADS * HEAD)
    gates = jax.nn.sigmoid(gate_logits.astype(jnp.float32))
    attended = (attention * lax.rsqrt(mean_square + 1e-06)[:, None] * norm_gain * gates).astype(
        jnp.bfloat16
    )
    summed = lax.psum_scatter(
        lax.dot_general(
            out_weight, attended, (((0,), (1,)), ((), ())), preferred_element_type=jnp.float32
        ).astype(jnp.bfloat16),
        "tp",
        scatter_dimension=0,
        tiled=True,
    ).astype(jnp.float32)
    return summed.T.astype(jnp.bfloat16)


def solution(mesh):
    return jax.shard_map(
        shards,
        mesh=mesh,
        in_specs=(
            P("seq", "tp"),
            P("seq", "tp"),
            P("seq", "tp"),
            P("tp", "seq"),
            P("seq", "tp"),
            P("tp"),
            P("tp", None),
        ),
        out_specs=P("seq", "tp"),
        check_vma=False,
    )
```

profile of v0, /device:TPU:1, one launch (start us, length us, event | category | flops | bytes accessed | tf_op | source)
XLA Modules:
  0.0 280.2 jit_solution(5316100465070949173)
XLA Ops:
  6.5 0.0 copy-start
  6.5 0.0 all-gather.3.cloned.1.call-start
  6.5 0.9 copy.38
  7.4 2.4 reduce-window.6
  9.8 0.1 slice.30
  9.9 0.1 copy.39
  10.0 0.1 copy.40
  10.1 0.1 broadcast_add_fusion
  10.2 0.1 slice.32
  10.3 0.1 copy.44
  10.4 0.1 copy.46
  10.5 0.1 exponential_bitcast_fusion.1
  10.6 2.4 reshape.88
  13.1 2.2 copy.45
  15.3 2.4 reshape.91
  17.7 1.3 dynamic-slice
  19.6 0.1 broadcast_multiply_fusion
  19.7 1.7 fusion.19
  21.5 0.0 copy-start.3
  21.5 0.8 copy-done.3
  22.3 0.8 slice_add_fusion
  23.1 0.0 all-gather.3.cloned.1.call-update
  23.1 0.0 reduce-scatter.4.cloned.1.call-start
  23.2 125.1 %all-reduce = f32[256]{0:T(256)S(1)} all-reduce(f32[256]{0:T(256)S(1)} %get-tuple-element.10), channel_id=2, replica_groups=mesh['seq'=64,'tp'=8] {'seq'}, use_global_device_ids=true, to_apply=%add | all-reduce | flops 256 | bytes 2048
  148.3 0.1 reshape.93
  148.4 0.1 reduce_window_sum.36
  148.5 0.1 select_bitcast_fusion
  148.6 0.1 copy.53
  148.7 2.5 reshape.87
  151.2 4.9 %fusion.3 = f32[2,4,384,128]{2,3,1,0:T(8,128)} fusion(f32[4,2,384]{2,0,1:T(4,128)S(1)} %copy.41, pred[384,384]{1,0:T(8,128)(4,1)S(1)} %iota_compare_fusion, bf16[2,384,4,128]{1,3,2,0:T(8,128)(2,1)} %copy.45, bf16[2,384,4,128]{3,2,1,0:T(4,128)(2,1)} %reshape.91, bf16[2,384,4,128]{3,2,1,0:T(4,128)(2,1)} %reshape.87), kind=kOutput, calls=%fused_computation.5 | convolution fusion | flops 609878016 | bytes 4091904 | tf_op jit(solution)/shard_map/hnts,nshb->nthb/dot_general | solution.py:28
  156.1 14.3 %all-gather.3.cloned.1.call-done = f32[64,4,128,128]{3,2,1,0:T(8,128)} async-done(((f32[1,4,128,128]{3,2,1,0:T(8,128)}), f32[64,4,128,128]{3,2,1,0:T(8,128)}) %all-gather.3.cloned.1.call-update) | async-done | bytes 16777232 | tf_op jit(solution)/shard_map/all_gather | solution.py:49
  170.3 0.0 copy-start.1
  170.3 0.0 copy-start.2
  170.4 22.7 %fusion = f32[4,1,128,128]{3,1,2,0:T(1,128)S(1)} fusion(f32[64,4,1,1]{0,2,3,1:T(1,128)S(1)} %copy.53, f32[64,4,128,128]{3,2,1,0:T(8,128)} %all-gather.3.cloned.1.call-done), kind=kOutput, calls=%fused_computation | convolution fusion | flops 50331648 | bytes 17040384 | tf_op jit(solution)/shard_map/mh,mhab->hab/dot_general | solution.py:56
  193.1 0.0 copy-done.4
  193.1 0.1 fusion.34
  193.2 0.0 copy-done.1
  193.2 0.0 copy-done.2
  193.2 3.5 %multiply_reduce_fusion = (f32[2,384]{1,0:T(2,128)S(1)}, f32[2,384,4,128]{1,3,2,0:T(8,128)}) fusion(f32[2,384,4]{1,2,0:T(4,128)S(1)} %copy.50, bf16[2,384,4,128]{3,2,1,0:T(4,128)(2,1)S(1)} %copy-done.1, f32[1,4,128,128]{3,2,1,0:T(8,128)S(1)} %fusion.34, f32[1,4,128,128]{3,2,1,0:T(8,128)S(1)} %bitcast.56, f32[2,4,384,128]{2,3,1,0:T(8,128)S(1)} %copy-done.2), kind=kOutput, calls=%fused_computation.16 | convolution fusion | flops 606076160 | bytes 4471808 | tf_op jit(solution)/shard_map/ntha,nhab->nthb/dot_general | solution.py:65
  196.7 2.6 copy.52
  199.4 25.9 %psum.7 = f32[768]{0:T(1024)S(1)} all-reduce(f32[768]{0:T(1024)S(1)} %reduce_sum.12), channel_id=1, replica_groups=mesh['seq'=64,'tp'=8] {'tp'}, use_global_device_ids=true, to_apply=%region_4.5 | all-reduce | flops 768 | bytes 6144 | tf_op jit(solution)/shard_map/psum | solution.py:67
  225.3 0.0 copy-done
  225.3 0.0 copy-done.5
  225.3 6.3 %fusion.2 = bf16[3072,768]{0,1:T(8,128)(2,1)} fusion(bf16[512,3072]{1,0:T(8,128)(2,1)S(1)} %copy-done, f32[96,8,4,128]{3,2,1,0:T(4,128)} %bitcast.57, bf16[768,512]{1,0:T(8,128)(2,1)} %param.11, f32[512]{0:T(512)S(1)} %copy-done.5, f32[768]{0:T(1024)S(1)} %add_rsqrt_fusion), kind=kOutput, calls=%fused_computation.4 | convolution fusion | flops 2421424128 | bytes 10228736 | tf_op jit(solution)/shard_map/dot_general | solution.py:74
  231.6 6.7 %copy.57 = bf16[3072,768]{1,0:T(8,128)(2,1)} copy(bf16[3072,768]{0,1:T(8,128)(2,1)} %fusion.2) | data formatting | bytes 9437184
  238.3 0.0 reduce-scatter.4.cloned.1.call-update
  238.4 32.9 %reduce-scatter.4.cloned.1.call-done = bf16[384,768]{1,0:T(8,128)(2,1)} async-done(((bf16[3072,768]{1,0:T(8,128)(2,1)}), bf16[384,768]{1,0:T(8,128)(2,1)}) %reduce-scatter.4.cloned.1.call-update) | async-done | bytes 589840
  271.3 2.1 copy.58
  (15 shorter events, 0.1 us)
Async XLA Ops:
  6.5 218.7 %copy-start = (bf16[512,3072]{1,0:T(8,128)(2,1)S(1)}, bf16[512,3072]{1,0:T(8,128)(2,1)}, u32[]{:S(2)}) copy-start(bf16[512,3072]{1,0:T(8,128)(2,1)} %param.13) | copy-start | bytes 9437188
  6.5 163.8 %all-gather.3.cloned.1.call-start = ((), (), s32[]{:S(2)}) async-start(), calls=%async_computation.1 | async-start | bytes 17039360 | tf_op jit(solution)/shard_map/all_gather | solution.py:49
  21.5 0.8 copy-start.3
  23.1 248.2 %reduce-scatter.4.cloned.1.call-start = ((), (), s32[]{:S(2)}) async-start(), calls=%async_computation.2 | async-start | bytes 5308416
  170.3 22.7 %copy-start.4 = (f32[2,4,128,128]{3,2,1,0:T(8,128)S(1)}, f32[2,4,128,128]{3,2,1,0:T(8,128)}, u32[]{:S(2)}) copy-start(f32[2,4,128,128]{3,2,1,0:T(8,128)} %copy-done.3) | copy-start | bytes 1572868
  170.3 22.8 %copy-start.1 = (bf16[2,384,4,128]{3,2,1,0:T(4,128)(2,1)S(1)}, bf16[2,384,4,128]{3,2,1,0:T(4,128)(2,1)}, u32[]{:S(2)}) copy-start(bf16[2,384,4,128]{3,2,1,0:T(4,128)(2,1)} %reshape.87) | copy-start | bytes 2359300
  170.3 22.8 %copy-start.2 = (f32[2,4,384,128]{2,3,1,0:T(8,128)S(1)}, f32[2,4,384,128]{2,3,1,0:T(8,128)}, u32[]{:S(2)}) copy-start(f32[2,4,384,128]{2,3,1,0:T(8,128)} %fusion.3) | copy-start | bytes 4718596
  196.7 28.5 %copy-start.5 = (f32[512]{0:T(512)S(1)}, f32[512]{0:T(512)}, u32[]{:S(2)}) copy-start(f32[512]{0:T(512)} %param.12) | copy-start | bytes 6148
Sparse Core Ops, SparseCore 0:
  23.2 147.0 all-gather.2
  238.5 32.7 reduce-scatter.3
where the time goes:
time: 282 us; the launch traced here: 280 us
  blocking collectives  151 us (54%)
  waiting for transfers between devices  47.2 us (17%)
  matrix products  39.2 us (14%)
  local copies, waits for them, and re-layouts  24.7 us (9%)
  between operations  14.2 us (5%)
  other arithmetic  3.83 us (1%)
    unnamed x1, blocking collectives  125 us
    unnamed x3, waiting for transfers between devices  33 us
    psum x1, blocking collectives, shards(): squares = lax.psum(jnp.sum(attention * attention, axis=1), 'tp')  25.9 us
    dot_general x1, matrix products, shards(): jnp.einsum('mh,mhab->hab', factors, portion, precision=lax.Precision.HIGH...  22.7 us
    all_gather x1, waiting for transfers between devices, shards(): portion = lax.all_gather(running[None], 'seq', axis=0, tiled=True)  14.3 us
    unnamed x16, local copies, waits for them, and re-layouts  10.9 us
    dot_general x1, matrix products, shards(): lax.dot_general(out_weight, attended, (((0,), (1,)), ((), ())), preferred...  6.33 us
  transfers between devices with their start and end apart: 2, of which 2 were waited for; matrix products, arithmetic and copies ran while one was open for 3% of the time, Pallas kernels for 0%

commit v1 on v0

--- a/solution.py
+++ b/solution.py
@@ -6,6 +6,33 @@
 HEAD = 128
 HEADS = 32
 BLOCK = 384
+
+
+def exchange(running, decay_sum):
+    head_count = running.shape[0]
+    ways = lax.axis_size("seq")
+    per_head = ways // head_count
+    rows = HEAD // per_head
+    pieces = running.astype(jnp.bfloat16).reshape(ways, rows, HEAD)
+    high = lax.reduce_precision(decay_sum, 8, 7)
+    middle = lax.reduce_precision(decay_sum - high, 8, 7)
+    low = lax.reduce_precision(decay_sum - high - middle, 8, 7)
+    parts = jnp.stack([high, middle, low] + [jnp.zeros_like(high)] * (rows - 3), axis=1)
+    parts = jnp.repeat(parts.astype(jnp.bfloat16), per_head, axis=0)
+    parts = jnp.broadcast_to(parts[:, :, None], (ways, rows, HEAD))
+    sent = jnp.concatenate([pieces, parts], axis=1)
+    got = lax.all_to_all(sent, "seq", 0, 0, tiled=True).astype(jnp.float32)
+    states = got[:, :rows].reshape(ways, rows * HEAD)
+    totals = jnp.sum(got[:, rows : rows + 3, 0], axis=1)
+    place = jnp.arange(ways)
+    target, origin, between = place[None, :, None], place[None, None, :], place[:, None, None]
+    inside = (between > origin) & (between < target)
+    spans = jnp.sum(jnp.where(inside, totals[:, None, None], 0.0), axis=0)
+    factors = jnp.where(place[None, :] < place[:, None], jnp.exp(spans), 0.0)
+    starts = jnp.dot(factors, states, precision=lax.Precision.HIGHEST)
+    back = starts.astype(jnp.bfloat16).reshape(ways, rows, HEAD)
+    mine = lax.all_to_all(back, "seq", 0, 0, tiled=True)
+    return mine.astype(jnp.float32).reshape(head_count, HEAD, HEAD)
 
 
 def shards(queries, key_rows, value_rows, log_decay, gate_logits, norm_gain, out_weight):
@@ -42,18 +69,7 @@
         decay_before.append(decay_sum)
         running = jnp.exp(totals[:, block])[:, None, None] * running + block_states[block]
         decay_sum = decay_sum + totals[:, block]
-    all_totals = lax.all_gather(decay_sum[None, :], "seq", axis=0, tiled=True)
-    inclusive = jnp.cumsum(all_totals, axis=0)
-    position = lax.axis_index("seq")
-    before_mine = lax.dynamic_index_in_dim(inclusive - all_totals, position, 0, keepdims=False)
-    portion = lax.all_gather(running[None], "seq", axis=0, tiled=True)
-    amount = portion.shape[0]
-    indices = jnp.arange(amount, dtype=jnp.int32)
-    earlier = (indices < position)[:, None]
-    factors = jnp.where(
-        earlier, jnp.exp(jnp.where(earlier, before_mine[None, :] - inclusive, 0.0)), 0.0
-    )
-    incoming = jnp.einsum("mh,mhab->hab", factors, portion, precision=lax.Precision.HIGHEST)
+    incoming = exchange(running, decay_sum)
     starts = jnp.stack(
         [
             jnp.exp(decay_before[block])[:, None, None] * incoming + local_before[block]
@@ -64,21 +80,21 @@
     scaled_queries = query_blocks.astype(jnp.float32) * query_scale
     carried = jnp.einsum("ntha,nhab->nthb", scaled_queries, starts, precision=lax.Precision.HIGHEST)
     attention = (inside + carried).reshape(rows_here, columns)
-    squares = lax.psum(jnp.sum(attention * attention, axis=1), "tp")
-    mean_square = squares / (HEADS * HEAD)
+    squares = jnp.sum(attention * attention, axis=1)
     gates = jax.nn.sigmoid(gate_logits.astype(jnp.float32))
-    attended = (attention * lax.rsqrt(mean_square + 1e-06)[:, None] * norm_gain * gates).astype(
-        jnp.bfloat16
-    )
+    attended = (attention * norm_gain * gates).astype(jnp.bfloat16)
+    ways = lax.axis_size("tp")
+    product = lax.dot_general(
+        out_weight, attended, (((0,), (1,)), ((), ())), preferred_element_type=jnp.float32
+    ).astype(jnp.bfloat16)
+    width = product.shape[0] // ways
+    extra = jnp.broadcast_to(squares.astype(jnp.bfloat16), (ways, 16, rows_here))
+    sent = jnp.concatenate([product.reshape(ways, width, rows_here), extra], axis=1)
     summed = lax.psum_scatter(
-        lax.dot_general(
-            out_weight, attended, (((0,), (1,)), ((), ())), preferred_element_type=jnp.float32
-        ).astype(jnp.bfloat16),
-        "tp",
-        scatter_dimension=0,
-        tiled=True,
+        sent.reshape(ways * (width + 16), rows_here), "tp", scatter_dimension=0, tiled=True
     ).astype(jnp.float32)
-    return summed.T.astype(jnp.bfloat16)
+    mean_square = summed[width] / (HEADS * HEAD)
+    return (summed[:width] * lax.rsqrt(mean_square + 1e-06)).T.astype(jnp.bfloat16)
 
 
 def solution(mesh):

time: 282 us -> 151 us (0.54)
  blocking collectives: 151 us -> 0 us
  starting transfers between devices: 0.04 us -> 23.2 us
  matrix products: 39.2 us -> 17.8 us
  other arithmetic: 3.83 us -> 14.9 us
  waiting for transfers between devices: 47.2 us -> 53 us
    unnamed x1 -> x0, blocking collectives: 125 us -> none
    reduce_scatter x0 -> x1, waiting for transfers between devices: none -> 38.4 us  [shards(): lax.psum_scatter(sent.reshape(ways * (width + 16), rows_here), 'tp', scat...]
    unnamed x3 -> x1, waiting for transfers between devices: 33 us -> 0.02 us
    psum x1 -> x0, blocking collectives: 25.9 us -> none  [shards(): squares = lax.psum(jnp.sum(attention * attention, axis=1), 'tp')]
    all_to_all x0 -> x2, starting transfers between devices: none -> 23 us  [the longest x1 17.1 us: exchange(): got = lax.all_to_all(sent, 'seq', 0, 0, tiled=True).astype(jnp.float32)]
    dot_general x1, matrix products: 22.7 us -> 0.25 us  [exchange(): starts = jnp.dot(factors, states, precision=lax.Precision.HIGHEST)]
    all_to_all x0 -> x2, waiting for transfers between devices: none -> 14.6 us  [the longest x1 8.22 us: exchange(): got = lax.all_to_all(sent, 'seq', 0, 0, tiled=True).astype(jnp.float32)]
    all_gather x1 -> x0, waiting for transfers between devices: 14.3 us -> none  [shards(): portion = lax.all_gather(running[None], 'seq', axis=0, tiled=True)]
  transfers between devices with their start and end apart: 2 -> 3, of which waited for: 2 -> 3; matrix products, arithmetic and copies ran while one was open for 3% -> 6% of each run, Pallas kernels for 0% -> 0%
where the time goes in v1:
time: 151 us; the launch traced here: 149 us
  waiting for transfers between devices  53 us (35%)
  local copies, waits for them, and re-layouts  26.2 us (17%)
  starting transfers between devices  23.2 us (15%)
  matrix products  17.8 us (12%)
  other arithmetic  14.9 us (10%)
  between operations  13.6 us (9%)
    reduce_scatter x1, waiting for transfers between devices, shards(): lax.psum_scatter(sent.reshape(ways * (width + 16), rows_here), 'tp', scat...  38.4 us
    all_to_all x1, starting transfers between devices, exchange(): got = lax.all_to_all(sent, 'seq', 0, 0, tiled=True).astype(jnp.float32)  17.1 us
    all_to_all x1, waiting for transfers between devices, exchange(): got = lax.all_to_all(sent, 'seq', 0, 0, tiled=True).astype(jnp.float32)  8.22 us
    reshape x1, local copies, waits for them, and re-layouts, shards(): product.reshape(ways, width, rows_here)  6.73 us
    all_to_all x1, waiting for transfers between devices, exchange(): mine = lax.all_to_all(back, 'seq', 0, 0, tiled=True)  6.36 us
    dot_general x1, matrix products, shards(): lax.dot_general(out_weight, attended, (((0,), (1,)), ((), ())), preferred...  6.01 us
    all_to_all x1, starting transfers between devices, exchange(): mine = lax.all_to_all(back, 'seq', 0, 0, tiled=True)  5.89 us
    dot_general x1, matrix products, shards(): jnp.einsum('ntha,nhab->nthb', scaled_queries, starts, precision=lax.Preci...  4.91 us
  transfers between devices with their start and end apart: 3, of which 3 were waited for; matrix products, arithmetic and copies ran while one was open for 6% of the time, Pallas kernels for 0%

profile of v1, /device:TPU:1, one launch (start us, length us, event | category | flops | bytes accessed | tf_op | source)
XLA Modules:
  0.0 148.7 jit_solution(12567551207518587956)
XLA Ops:
  6.5 0.9 copy.46
  7.4 2.4 %reduce-window.6 = f32[4,2,3,128]{3,2,1,0:T(4,128)S(1)} reduce-window(f32[4,2,3,128]{3,2,1,0:T(4,128)S(1)} %copy.46, f32[]{:T(128)} %constant.5.clone.1), window={size=1x1x1x128 pad=0_0x0_0x0_0x127_0}, to_apply=%region_0.0 | reduce-window | flops 390144 | bytes 24580 | tf_op jit(solution)/shard_map/reduce-window
  9.8 0.1 slice.50
  9.9 0.1 copy.47
  10.0 0.1 copy.48
  10.1 0.1 broadcast_add_fusion
  10.3 0.1 copy.52
  10.4 0.1 copy.54
  10.5 0.6 fusion.43
  11.2 0.1 mul.93
  11.2 0.1 copy.59
  11.4 0.1 copy.58
  11.5 0.1 copy.57
  11.6 0.1 mul.89
  11.7 0.1 exponential_bitcast_fusion.1
  11.8 2.5 %reshape.128 = bf16[2,384,4,128]{3,2,1,0:T(4,128)(2,1)} reshape(bf16[768,512]{1,0:T(8,128)(2,1)} %param.9) | data formatting | bytes 1572864 | tf_op jit(solution)/shard_map/reshape | solution.py:45
  14.3 2.4 %reshape.125 = bf16[2,384,4,128]{3,2,1,0:T(4,128)(2,1)} reshape(bf16[768,512]{1,0:T(8,128)(2,1)} %param.8) | data formatting | bytes 1572864 | tf_op jit(solution)/shard_map/reshape | solution.py:44
  16.7 2.2 %copy.53 = bf16[2,384,4,128]{1,3,2,0:T(8,128)(2,1)} copy(bf16[2,384,4,128]{3,2,1,0:T(4,128)(2,1)} %reshape.125) | data formatting | bytes 1572864 | tf_op jit(solution)/shard_map/reshape | solution.py:44
  18.9 1.7 %fusion.17 = f32[2,4,128,128]{3,2,1,0:T(8,128)S(1)} fusion(bf16[2,384,4,128]{1,3,2,0:T(8,128)(2,1)} %copy.53, f32[2,384,4]{1,2,0:T(4,128)S(1)} %copy.55, bf16[2,384,4,128]{3,2,1,0:T(4,128)(2,1)} %reshape.128), kind=kOutput, calls=%fused_computation.24 | convolution fusion | flops 101842944 | bytes 2109440 | tf_op jit(solution)/shard_map/ntha,nthb->nhab/dot_general | solution.py:60
  20.7 0.8 copy-done.2
  21.5 0.2 add_convert_fusion
  21.7 0.1 stack.5
  21.8 0.1 broadcast_in_dim.67
  22.0 0.7 pad_maximum_fusion.1
  22.7 17.1 %all-to-all-start = ((bf16[64,16,128]{2,1,0:T(8,128)(2,1)}), bf16[64,16,128]{2,1,0:T(8,128)(2,1)S(1)}, u32[]{:S(2)}, u32[]{:S(2)}) async-start(bf16[64,16,128]{2,1,0:T(8,128)(2,1)} %pad_maximum_fusion.1), calls=%async_computation | async-start | bytes 524288 | tf_op jit(solution)/shard_map/all_to_all | solution.py:24
  39.9 0.6 copy.49
  40.5 0.6 copy.61
  41.1 2.5 %reshape.124 = bf16[2,384,4,128]{3,2,1,0:T(4,128)(2,1)} reshape(bf16[768,512]{1,0:T(8,128)(2,1)} %param.7) | data formatting | bytes 1572864 | tf_op jit(solution)/shard_map/reshape | solution.py:43
  43.5 0.6 iota_compare_fusion.1
  44.2 8.2 %all-to-all-done = bf16[64,16,128]{2,1,0:T(8,128)(2,1)S(1)} async-done(((bf16[64,16,128]{2,1,0:T(8,128)(2,1)}), bf16[64,16,128]{2,1,0:T(8,128)(2,1)S(1)}, u32[]{:S(2)}, u32[]{:S(2)}) %all-to-all-start) | async-done | bytes 262176 | tf_op jit(solution)/shard_map/all_to_all | solution.py:24
  52.4 0.6 convert_reduce_fusion
  53.0 1.5 %select_reduce_fusion = f32[64,64]{1,0:T(8,128)S(1)} fusion(f32[64]{0:T(128)S(1)} %convert_reduce_fusion, pred[64,64]{1,0:T(8,128)(4,1)} %get-tuple-element.17, pred[64,64]{1,0:T(8,128)(4,1)} %get-tuple-element.18), kind=kLoop, calls=%fused_computation.10 | loop fusion | flops 782336 | bytes 24832 | tf_op jit(solution)/shard_map/reduce_sum | solution.py:30
  54.5 0.3 fusion.16
  54.8 0.7 copy.69
  55.4 5.9 %all-to-all-start.1 = ((bf16[64,8,128]{2,1,0:T(8,128)(2,1)}), bf16[64,8,128]{2,1,0:T(8,128)(2,1)S(1)}, u32[]{:S(2)}, u32[]{:S(2)}) async-start(bf16[64,8,128]{2,1,0:T(8,128)(2,1)} %bitcast.21), calls=%async_computation.1 | async-start | bytes 262144 | tf_op jit(solution)/shard_map/all_to_all | solution.py:34
  61.4 0.2 reduce-scatter.2.cloned.1.call-start
  61.6 4.9 %fusion.1 = f32[2,4,384,128]{2,3,1,0:T(8,128)} fusion(f32[4,2,384]{2,0,1:T(4,128)} %copy.49, pred[384,384]{1,0:T(8,128)(4,1)S(1)} %iota_compare_fusion, bf16[2,384,4,128]{1,3,2,0:T(8,128)(2,1)} %copy.53, bf16[2,384,4,128]{3,2,1,0:T(4,128)(2,1)} %reshape.128, bf16[2,384,4,128]{3,2,1,0:T(4,128)(2,1)} %reshape.124), kind=kOutput, calls=%fused_computation.4 | convolution fusion | flops 609878016 | bytes 4091904 | tf_op jit(solution)/shard_map/hnts,nshb->nthb/dot_general | solution.py:55
  66.5 6.4 %all-to-all-done.1 = bf16[64,8,128]{2,1,0:T(8,128)(2,1)S(1)} async-done(((bf16[64,8,128]{2,1,0:T(8,128)(2,1)}), bf16[64,8,128]{2,1,0:T(8,128)(2,1)S(1)}, u32[]{:S(2)}, u32[]{:S(2)}) %all-to-all-start.1) | async-done | bytes 131104 | tf_op jit(solution)/shard_map/all_to_all | solution.py:34
  72.9 1.1 add_add_fusion
  74.0 4.9 %multiply_reduce_fusion = (bf16[2,384]{1,0:T(2,128)(2,1)S(1)}, f32[2,384,4,128]{1,3,2,0:T(8,128)}) fusion(f32[2,384,4]{1,2,0:T(4,128)S(1)} %copy-done.3, bf16[2,384,4,128]{3,2,1,0:T(4,128)(2,1)S(1)} %copy-done.1, f32[1,4,128,128]{3,2,1,0:T(8,128)S(1)} %add_add_fusion, f32[1,4,128,128]{3,2,1,0:T(8,128)S(1)} %convert.18, f32[2,4,384,128]{2,3,1,0:T(8,128)} %fusion.1), kind=kOutput, calls=%fused_computation.15 | convolution fusion | flops 606076160 | bytes 4470272 | tf_op jit(solution)/shard_map/ntha,nhab->nthb/dot_general | solution.py:81
  79.0 2.6 %copy.63 = f32[2,384,4,128]{3,2,1,0:T(4,128)} copy(f32[2,384,4,128]{1,3,2,0:T(8,128)} %get-tuple-element.16) | data formatting | bytes 3145728 | tf_op jit(solution)/shard_map/add | solution.py:82
  81.6 6.0 %fusion = bf16[3072,768]{0,1:T(8,128)(2,1)} fusion(bf16[512,3072]{1,0:T(8,128)(2,1)S(1)} %copy-done, f32[96,8,4,128]{3,2,1,0:T(4,128)} %bitcast.50, bf16[768,512]{1,0:T(8,128)(2,1)} %param.11, f32[512]{0:T(512)S(1)} %copy-done.7), kind=kOutput, calls=%fused_computation.3 | convolution fusion | flops 2421030912 | bytes 10225664 | tf_op jit(solution)/shard_map/dot_general | solution.py:87
  87.6 6.7 %copy.67 = bf16[3072,768]{1,0:T(8,128)(2,1)} copy(bf16[3072,768]{0,1:T(8,128)(2,1)} %fusion) | data formatting | bytes 9437184 | tf_op jit(solution)/shard_map/reshape | solution.py:92
  94.4 4.8 %pad_maximum_fusion = bf16[8,400,768]{2,1,0:T(8,128)(2,1)} fusion(bf16[8,16,768]{2,1,0:T(8,128)(2,1)S(1)} %broadcast_in_dim.71, bf16[8,384,768]{2,1,0:T(8,128)(2,1)} %bitcast.49), kind=kLoop, calls=%fused_computation.1 | loop fusion | flops 9830400 | bytes 9830400 | tf_op jit(solution)/shard_map/concatenate | solution.py:92
  99.2 38.4 %reduce-scatter.2.cloned.1.call-done = bf16[400,768]{1,0:T(8,128)(2,1)} async-done(((bf16[3200,768]{1,0:T(8,128)(2,1)}), bf16[400,768]{1,0:T(8,128)(2,1)}) %reduce-scatter.2.cloned.1.call-update) | async-done | bytes 614416 | tf_op jit(solution)/shard_map/reduce_scatter | solution.py:93
  137.7 1.2 convert_element_type.61
  138.9 0.9 fusion.28
  139.7 2.1 %copy.65 = bf16[768,384]{1,0:T(8,128)(2,1)} copy(bf16[768,384]{0,1:T(8,128)(2,1)} %fusion.28) | data formatting | bytes 1179648 | tf_op jit(solution)/shard_map/convert_element_type | solution.py:97
  (35 shorter events, 0.5 us)
Async XLA Ops:
  6.5 75.1 %copy-start = (bf16[512,3072]{1,0:T(8,128)(2,1)S(1)}, bf16[512,3072]{1,0:T(8,128)(2,1)}, u32[]{:S(2)}) copy-start(bf16[512,3072]{1,0:T(8,128)(2,1)} %param.13) | copy-start | bytes 9437188
  10.4 1.4 copy-start.4
  20.7 0.8 copy-start.2
  22.7 29.7 %all-to-all-start = ((bf16[64,16,128]{2,1,0:T(8,128)(2,1)}), bf16[64,16,128]{2,1,0:T(8,128)(2,1)S(1)}, u32[]{:S(2)}, u32[]{:S(2)}) async-start(bf16[64,16,128]{2,1,0:T(8,128)(2,1)} %pad_maximum_fusion.1), calls=%async_computation | async-start | bytes 524288 | tf_op jit(solution)/shard_map/all_to_all | solution.py:24
  55.4 17.4 %all-to-all-start.1 = ((bf16[64,8,128]{2,1,0:T(8,128)(2,1)}), bf16[64,8,128]{2,1,0:T(8,128)(2,1)S(1)}, u32[]{:S(2)}, u32[]{:S(2)}) async-start(bf16[64,8,128]{2,1,0:T(8,128)(2,1)} %bitcast.21), calls=%async_computation.1 | async-start | bytes 262144 | tf_op jit(solution)/shard_map/all_to_all | solution.py:34
  61.3 11.5 %copy-start.5 = (f32[4]{0:T(128)S(1)}, f32[4]{0:T(128)}, u32[]{:S(2)}) copy-start(f32[4]{0:T(128)} %copy-done.4) | copy-start | bytes 52
  61.3 11.5 %copy-start.6 = (f32[4]{0:T(128)S(1)}, f32[4]{0:T(128)}, u32[]{:S(2)}) copy-start(f32[4]{0:T(128)} %get-tuple-element.12) | copy-start | bytes 52
  61.3 12.7 %copy-start.3 = (f32[2,384,4]{1,2,0:T(4,128)S(1)}, f32[2,384,4]{1,2,0:T(4,128)}, u32[]{:S(2)}) copy-start(f32[2,384,4]{1,2,0:T(4,128)} %copy.61) | copy-start | bytes 36868
  61.4 76.3 %reduce-scatter.2.cloned.1.call-start = ((), (), s32[]{:S(2)}) async-start(), calls=%async_computation.3 | async-start | bytes 5529600 | tf_op jit(solution)/shard_map/reduce_scatter | solution.py:93
  72.8 1.2 copy-start.1
  79.0 2.6 %copy-start.7 = (f32[512]{0:T(512)S(1)}, f32[512]{0:T(512)}, u32[]{:S(2)}) copy-start(f32[512]{0:T(512)} %param.12) | copy-start | bytes 6148
Sparse Core Ops, SparseCore 0:
  99.4 38.2 reduce-scatter.1

commit v2 on v1

--- a/solution.py
+++ b/solution.py
@@ -1,6 +1,8 @@
 import jax
 import jax.numpy as jnp
 from jax import lax
+from jax.experimental import pallas as pl
+from jax.experimental.pallas import tpu as pltpu
 from jax.sharding import PartitionSpec as P
 
 HEAD = 128
@@ -35,6 +37,173 @@
     return mine.astype(jnp.float32).reshape(head_count, HEAD, HEAD)
 
 
+def project_kernel(
+    a_ref, w_ref, sq_ref, o_ref,
+    give, got, held, own, relay, landed, squares,
+    give_send, give_recv, far_send, far_recv, near_send, near_recv,
+    last_send, last_recv, sq_send, sq_recv,
+):
+    tokens, width = o_ref.shape
+    half = tokens // 2
+    tile = tokens // 3
+    me = lax.axis_index("tp")
+    core = lax.rem(me, 2)
+    chip = lax.div(me, 2)
+
+    def device(step, which):
+        return lax.rem(chip + step, 4) * 2 + which
+
+    sibling = device(0, 1 - core)
+    right, left = device(1, core), device(3, core)
+
+    barrier = pltpu.get_barrier_semaphore()
+    for offset in range(1, 8):
+        pl.semaphore_signal(
+            barrier, inc=1, device_id={"tp": lax.rem(me + offset, 8)},
+            device_id_type=pl.DeviceIdType.MESH,
+        )
+    pl.semaphore_wait(barrier, 7)
+
+    def send(source, target, send_sem, recv_sem, to):
+        copy = pltpu.make_async_remote_copy(
+            src_ref=source, dst_ref=target, send_sem=send_sem, recv_sem=recv_sem,
+            device_id={"tp": to}, device_id_type=pl.DeviceIdType.MESH,
+        )
+        copy.start()
+        return copy
+
+    copies = []
+    sq_copies = [
+        send(sq_ref, squares.at[i], sq_send.at[i], sq_recv.at[i], lax.rem(me + i + 1, 8))
+        for i in range(7)
+    ]
+
+    def tiles(body):
+        def step(i, carry):
+            body(pl.ds(pl.multiple_of(i * tile, tile), tile))
+            return carry
+
+        lax.fori_loop(0, 3, step, 0)
+
+    def product(dest, rows):
+        columns = pl.ds(pl.multiple_of(dest * width, 128), width)
+        return jnp.dot(a_ref[rows, :], w_ref[:, columns], preferred_element_type=jnp.float32)
+
+    steps = (2, 1, 3, 0)
+    gives = []
+
+    def hand_over(k):
+        def body(rows):
+            give[k, rows, :] = product(device(steps[k], 1 - core), rows).astype(jnp.bfloat16)
+
+        tiles(body)
+        gives.append(send(give.at[k], got.at[k], give_send.at[k], give_recv.at[k], sibling))
+
+    def gather(k, target, dtype):
+        def first(rows):
+            own[rows, :] = product(device(steps[k], core), rows)
+
+        tiles(first)
+        gives[k].wait_recv()
+
+        def second(rows):
+            total = own[rows, :] + got[k, rows, :].astype(jnp.float32)
+            if dtype is None:
+                own[rows, :] = total
+            else:
+                target[k, rows, :] = total.astype(dtype)
+
+        tiles(second)
+
+    top, bottom = pl.ds(0, half), pl.ds(half, half)
+    hand_over(0)
+    hand_over(1)
+    gather(0, held, jnp.bfloat16)
+    far_right = send(held.at[0, top], relay.at[0], far_send.at[0], far_recv.at[0], right)
+    far_left = send(held.at[0, bottom], relay.at[1], far_send.at[1], far_recv.at[1], left)
+    hand_over(2)
+    gather(1, held, jnp.bfloat16)
+    near_right = send(
+        held.at[1, bottom], landed.at[0, bottom], near_send.at[0], near_recv.at[0], right
+    )
+    hand_over(3)
+    gather(2, held, jnp.bfloat16)
+    near_left = send(held.at[2, top], landed.at[1, top], near_send.at[1], near_recv.at[1], left)
+    gather(3, None, None)
+
+    def merge(k, start, slot):
+        piece = half // 3
+
+        def step(i, carry):
+            rows = pl.ds(pl.multiple_of(start + i * piece, piece), piece)
+            here = pl.ds(pl.multiple_of(i * piece, piece), piece)
+            total = held[k, rows, :].astype(jnp.float32) + relay[slot, here, :].astype(jnp.float32)
+            held[k, rows, :] = total.astype(jnp.bfloat16)
+            return carry
+
+        lax.fori_loop(0, 3, step, 0)
+
+    far_right.wait_recv()
+    merge(1, 0, 0)
+    last_right = send(held.at[1, top], landed.at[0, top], last_send.at[0], last_recv.at[0], right)
+    far_left.wait_recv()
+    merge(2, half, 1)
+    last_left = send(
+        held.at[2, bottom], landed.at[1, bottom], last_send.at[1], last_recv.at[1], left
+    )
+    total = sq_ref[...]
+    for i in range(7):
+        sq_copies[i].wait_recv()
+        total = total + squares[i]
+    scale = lax.rsqrt(total / (HEADS * HEAD) + 1e-06)
+    scale = jnp.transpose(jnp.broadcast_to(scale, (8, tokens)))[:, :1]
+    near_right.wait_recv()
+    near_left.wait_recv()
+    last_right.wait_recv()
+    last_left.wait_recv()
+    for i in range(3):
+        rows = slice(i * tile, (i + 1) * tile)
+        summed = (
+            own[rows, :]
+            + landed[0, rows, :].astype(jnp.float32)
+            + landed[1, rows, :].astype(jnp.float32)
+        )
+        o_ref[rows, :] = (summed * scale[rows]).astype(o_ref.dtype)
+    for copy in sq_copies + gives + [
+        far_right, far_left, near_right, near_left, last_right, last_left
+    ]:
+        copy.wait_send()
+
+
+def project(attended, out_weight, squares):
+    tokens = attended.shape[0]
+    width = out_weight.shape[1] // 8
+    block = (4, tokens, width)
+    pair = pltpu.SemaphoreType.DMA((2,))
+    four = pltpu.SemaphoreType.DMA((4,))
+    seven = pltpu.SemaphoreType.DMA((7,))
+    vmem = pl.BlockSpec(memory_space=pltpu.VMEM)
+    return pl.pallas_call(
+        project_kernel,
+        out_shape=jax.ShapeDtypeStruct((tokens, width), jnp.bfloat16),
+        in_specs=[vmem] * 3,
+        out_specs=vmem,
+        scratch_shapes=[
+            pltpu.VMEM(block, jnp.bfloat16),
+            pltpu.VMEM(block, jnp.bfloat16),
+            pltpu.VMEM((3, tokens, width), jnp.bfloat16),
+            pltpu.VMEM((tokens, width), jnp.float32),
+            pltpu.VMEM((2, tokens // 2, width), jnp.bfloat16),
+            pltpu.VMEM((2, tokens, width), jnp.bfloat16),
+            pltpu.VMEM((7, 1, tokens), jnp.float32),
+            four, four, pair, pair, pair, pair, pair, pair, seven, seven,
+        ],
+        compiler_params=pltpu.CompilerParams(
+            collective_id=0, has_side_effects=True, vmem_limit_bytes=40 << 20
+        ),
+    )(attended, out_weight, squares)
+
+
 def shards(queries, key_rows, value_rows, log_decay, gate_logits, norm_gain, out_weight):
     rows_here = queries.shape[0]
     columns = queries.shape[1]
@@ -83,18 +252,7 @@
     squares = jnp.sum(attention * attention, axis=1)
     gates = jax.nn.sigmoid(gate_logits.astype(jnp.float32))
     attended = (attention * norm_gain * gates).astype(jnp.bfloat16)
-    ways = lax.axis_size("tp")
-    product = lax.dot_general(
-        out_weight, attended, (((0,), (1,)), ((), ())), preferred_element_type=jnp.float32
-    ).astype(jnp.bfloat16)
-    width = product.shape[0] // ways
-    extra = jnp.broadcast_to(squares.astype(jnp.bfloat16), (ways, 16, rows_here))
-    sent = jnp.concatenate([product.reshape(ways, width, rows_here), extra], axis=1)
-    summed = lax.psum_scatter(
-        sent.reshape(ways * (width + 16), rows_here), "tp", scatter_dimension=0, tiled=True
-    ).astype(jnp.float32)
-    mean_square = summed[width] / (HEADS * HEAD)
-    return (summed[:width] * lax.rsqrt(mean_square + 1e-06)).T.astype(jnp.bfloat16)
+    return project(attended, out_weight, squares[None, :])
 
 
 def solution(mesh):

time: 151 us -> 99.3 us (0.66); the launches traced: 149 us -> 98.9 us
  waiting for transfers between devices: 53 us -> 19.2 us
  Pallas kernels: 0 us -> 30.9 us
  local copies, waits for them, and re-layouts: 26.2 us -> 8.61 us
  between operations: 13.6 us -> 0.27 us
  other arithmetic: 14.9 us -> 6.86 us
  matrix products: 17.8 us -> 9.92 us
    reduce_scatter x1 -> x0, waiting for transfers between devices: 38.4 us -> none  [shards(): lax.psum_scatter(sent.reshape(ways * (width + 16), rows_here), 'tp', scat...]
    pallas_call x0 -> x1, Pallas kernels: none -> 30.9 us  [project(): pl.pallas_call(project_kernel, out_shape=jax.ShapeDtypeStruct((tokens, wi...]
    reshape x2 -> x1, local copies, waits for them, and re-layouts: 7.59 us -> 0.71 us  [the longest x1 6.73 us: shards(): product.reshape(ways, width, rows_here)]
    dot_general x1 -> x0, matrix products: 6.01 us -> none  [shards(): lax.dot_general(out_weight, attended, (((0,), (1,)), ((), ())), preferred...]
    concatenate x1 -> x0, other arithmetic: 4.85 us -> none  [shards(): jnp.concatenate([product.reshape(ways, width, rows_here), extra], axis=1)]
    all_to_all x1, waiting for transfers between devices: 8.22 us -> 12.3 us  [exchange(): got = lax.all_to_all(sent, 'seq', 0, 0, tiled=True).astype(jnp.float32)]
    reshape x1, local copies, waits for them, and re-layouts: 2.47 us -> 0.18 us  [shards(): query_blocks = queries.reshape(blocks, BLOCK, head_count, HEAD)]
    reshape x2, local copies, waits for them, and re-layouts: 4.62 us -> 2.45 us  [shards(): key_blocks = key_rows.reshape(blocks, BLOCK, head_count, HEAD)]
  transfers between devices with their start and end apart: 3 -> 2, of which waited for: 3 -> 2; matrix products, arithmetic and copies ran while one was open for 6% -> 5% of each run, Pallas kernels for 0% -> 0%
where the time goes in v2:
time: 99.3 us; the launch traced here: 98.9 us
  Pallas kernels  30.9 us (31%)
  starting transfers between devices  23.2 us (23%)
  waiting for transfers between devices  19.2 us (19%)
  matrix products  9.92 us (10%)
  local copies, waits for them, and re-layouts  8.61 us (9%)
  other arithmetic  6.86 us (7%)
    pallas_call x1, Pallas kernels, project(): pl.pallas_call(project_kernel, out_shape=jax.ShapeDtypeStruct((tokens, wi...  30.9 us
    all_to_all x1, starting transfers between devices, exchange(): got = lax.all_to_all(sent, 'seq', 0, 0, tiled=True).astype(jnp.float32)  17.1 us
    all_to_all x1, waiting for transfers between devices, exchange(): got = lax.all_to_all(sent, 'seq', 0, 0, tiled=True).astype(jnp.float32)  12.3 us
    all_to_all x1, waiting for transfers between devices, exchange(): mine = lax.all_to_all(back, 'seq', 0, 0, tiled=True)  6.92 us
    all_to_all x1, starting transfers between devices, exchange(): mine = lax.all_to_all(back, 'seq', 0, 0, tiled=True)  6.06 us
    dot_general x1, matrix products, shards(): jnp.einsum('hnts,nshb->nthb', weighted, value_blocks, preferred_element_t...  4.4 us
    dot_general x1, matrix products, shards(): jnp.einsum('ntha,nhab->nthb', scaled_queries, starts, precision=lax.Preci...  3.76 us
    another operation x5, other arithmetic  2.51 us
  transfers between devices with their start and end apart: 2, of which 2 were waited for; matrix products, arithmetic and copies ran while one was open for 5% of the time, Pallas kernels for 0%

profile of v2, /device:TPU:1, one launch (start us, length us, event | category | flops | bytes accessed | tf_op | source)
XLA Modules:
  0.0 98.9 jit_solution(9811216859164679817)
XLA Ops:
  0.0 0.7 copy.45
  0.7 2.4 %reduce-window.6 = f32[4,2,3,128]{3,2,1,0:T(4,128)S(1)} reduce-window(f32[4,2,3,128]{3,2,1,0:T(4,128)S(1)} %copy.45, f32[]{:T(128)} %constant.4.clone.1), window={size=1x1x1x128 pad=0_0x0_0x0_0x127_0}, to_apply=%region_0.0 | reduce-window | flops 390144 | bytes 24580 | tf_op jit(solution)/shard_map/reduce-window
  3.1 0.1 slice.42
  3.2 0.1 copy.46
  3.3 0.1 copy.47
  3.4 0.1 broadcast_add_fusion
  3.5 0.1 slice.44
  3.6 0.1 copy.51
  3.7 0.1 copy.53
  3.8 0.1 exponential_bitcast_fusion.1
  3.9 0.0 copy-start.1
  4.0 1.8 %reshape.119 = bf16[2,384,4,128]{3,2,1,0:T(4,128)(2,1)S(1)} reshape(bf16[768,512]{1,0:T(8,128)(2,1)} %param.8) | data formatting | bytes 1572864 | tf_op jit(solution)/shard_map/reshape | solution.py:213
  5.8 0.6 copy.52
  6.4 0.0 copy-done.1
  6.4 1.1 %reshape.122 = bf16[2,384,4,128]{3,2,1,0:T(4,128)(2,1)} reshape(bf16[768,512]{1,0:T(8,128)(2,1)S(1)} %copy-done.1) | data formatting | bytes 1572864 | tf_op jit(solution)/shard_map/reshape | solution.py:214
  7.5 1.5 %fusion.15 = f32[2,4,128,128]{3,2,1,0:T(8,128)S(1)} fusion(bf16[2,384,4,128]{1,3,2,0:T(8,128)(2,1)S(1)} %copy.52, f32[2,384,4]{1,2,0:T(4,128)S(1)} %copy.54, bf16[2,384,4,128]{3,2,1,0:T(4,128)(2,1)} %reshape.122), kind=kOutput, calls=%fused_computation.19 | convolution fusion | flops 101842944 | bytes 2109440 | tf_op jit(solution)/shard_map/ntha,nthb->nhab/dot_general | solution.py:229
  9.0 0.0 copy-start.2
  9.1 0.1 mul.78
  9.1 0.1 mul.79
  9.2 0.1 mul.82
  9.3 0.1 mul.83
  9.4 0.1 copy.56
  9.5 0.1 copy.57
  9.6 0.1 copy.58
  9.7 0.2 add_convert_fusion
  9.9 0.1 stack.5
  10.0 0.1 broadcast_in_dim.66
  10.2 0.7 pad_maximum_fusion
  10.9 17.1 %all-to-all-start = ((bf16[64,16,128]{2,1,0:T(8,128)(2,1)}), bf16[64,16,128]{2,1,0:T(8,128)(2,1)S(1)}, u32[]{:S(2)}, u32[]{:S(2)}) async-start(bf16[64,16,128]{2,1,0:T(8,128)(2,1)} %pad_maximum_fusion), calls=%async_computation | async-start | bytes 524288 | tf_op jit(solution)/shard_map/all_to_all | solution.py:26
  28.1 0.0 copy-done.2
  28.1 0.2 reshape.118
  28.4 12.3 %all-to-all-done = bf16[64,16,128]{2,1,0:T(8,128)(2,1)S(1)} async-done(((bf16[64,16,128]{2,1,0:T(8,128)(2,1)}), bf16[64,16,128]{2,1,0:T(8,128)(2,1)S(1)}, u32[]{:S(2)}, u32[]{:S(2)}) %all-to-all-start) | async-done | bytes 262176 | tf_op jit(solution)/shard_map/all_to_all | solution.py:26
  40.6 0.6 convert_reduce_fusion
  41.2 0.8 select_reduce_fusion
  42.0 0.3 fusion.14
  42.3 0.7 copy.65
  43.0 6.1 %all-to-all-start.1 = ((bf16[64,8,128]{2,1,0:T(8,128)(2,1)}), bf16[64,8,128]{2,1,0:T(8,128)(2,1)S(1)}, u32[]{:S(2)}, u32[]{:S(2)}) async-start(bf16[64,8,128]{2,1,0:T(8,128)(2,1)} %bitcast.17), calls=%async_computation.1 | async-start | bytes 262144 | tf_op jit(solution)/shard_map/all_to_all | solution.py:36
  49.0 4.4 %fusion = f32[2,4,384,128]{2,3,1,0:T(8,128)} fusion(f32[4,2,384]{2,0,1:T(4,128)S(1)} %copy.48, pred[384,384]{1,0:T(8,128)(4,1)S(1)} %iota_compare_fusion, bf16[2,384,4,128]{1,3,2,0:T(8,128)(2,1)S(1)} %copy.52, bf16[2,384,4,128]{3,2,1,0:T(4,128)(2,1)} %reshape.122, bf16[2,384,4,128]{3,2,1,0:T(4,128)(2,1)S(1)} %reshape.118), kind=kOutput, calls=%fused_computation.1 | convolution fusion | flops 609878016 | bytes 4091904 | tf_op jit(solution)/shard_map/hnts,nshb->nthb/dot_general | solution.py:224
  53.4 6.9 %all-to-all-done.1 = bf16[64,8,128]{2,1,0:T(8,128)(2,1)S(1)} async-done(((bf16[64,8,128]{2,1,0:T(8,128)(2,1)}), bf16[64,8,128]{2,1,0:T(8,128)(2,1)S(1)}, u32[]{:S(2)}, u32[]{:S(2)}) %all-to-all-start.1) | async-done | bytes 131104 | tf_op jit(solution)/shard_map/all_to_all | solution.py:36
  60.4 0.1 add_add_fusion
  60.5 3.8 %multiply_reduce_fusion = (f32[2,384]{1,0:T(2,128)S(1)}, f32[2,384,4,128]{1,3,2,0:T(8,128)S(1)}) fusion(f32[2,384,4]{1,2,0:T(4,128)S(1)} %copy.60, bf16[2,384,4,128]{3,2,1,0:T(4,128)(2,1)S(1)} %reshape.118, f32[1,4,128,128]{3,2,1,0:T(8,128)S(1)} %add_add_fusion, f32[1,4,128,128]{3,2,1,0:T(8,128)S(1)} %convert.18, f32[2,4,384,128]{2,3,1,0:T(8,128)} %fusion), kind=kOutput, calls=%fused_computation.12 | convolution fusion | flops 606076160 | bytes 4471808 | tf_op jit(solution)/shard_map/ntha,nhab->nthb/dot_general | solution.py:250
  64.3 0.0 copy-start.3
  64.3 0.8 copy.62
  65.1 0.0 copy-start
  65.1 1.7 %fusion.8.a_ref = bf16[768,512]{1,0:T(8,128)(2,1)S(1)} fusion(f32[96,8,4,128]{3,2,1,0:T(4,128)S(1)} %bitcast.44, bf16[768,512]{1,0:T(8,128)(2,1)} %param.11, f32[512]{0:T(512)S(1)} %copy-done.3), kind=kLoop, calls=%fused_computation.10 | loop fusion | flops 2752512 | bytes 3147776 | tf_op jit(solution)/shard_map/convert_element_type | solution.py:254
  66.8 0.4 copy-done
  67.2 30.9 %shard_map.73 = bf16[768,384]{1,0:T(8,128)(2,1)S(1)} custom-call(bf16[768,512]{1,0:T(8,128)(2,1)S(1)} %fusion.8.a_ref, bf16[512,3072]{1,0:T(8,128)(2,1)S(1)} %copy-done, f32[1,768]{1,0:T(1,128)S(1)} %bitcast.43), custom_call_target="tpu_custom_call" | custom-call | tf_op jit(solution)/shard_map/pallas_call | solution.py:186
  98.1 0.8 copy.87
  (19 shorter events, 0.2 us)
Async XLA Ops:
  3.9 2.5 %copy-start.1 = (bf16[768,512]{1,0:T(8,128)(2,1)S(1)}, bf16[768,512]{1,0:T(8,128)(2,1)}, u32[]{:S(2)}) copy-start(bf16[768,512]{1,0:T(8,128)(2,1)} %param.9) | copy-start | bytes 2359300
  9.0 19.1 %copy-start.2 = (bf16[768,512]{1,0:T(8,128)(2,1)S(1)}, bf16[768,512]{1,0:T(8,128)(2,1)}, u32[]{:S(2)}) copy-start(bf16[768,512]{1,0:T(8,128)(2,1)} %param.7) | copy-start | bytes 2359300
  10.9 29.7 %all-to-all-start = ((bf16[64,16,128]{2,1,0:T(8,128)(2,1)}), bf16[64,16,128]{2,1,0:T(8,128)(2,1)S(1)}, u32[]{:S(2)}, u32[]{:S(2)}) async-start(bf16[64,16,128]{2,1,0:T(8,128)(2,1)} %pad_maximum_fusion), calls=%async_computation | async-start | bytes 524288 | tf_op jit(solution)/shard_map/all_to_all | solution.py:26
  43.0 17.4 %all-to-all-start.1 = ((bf16[64,8,128]{2,1,0:T(8,128)(2,1)}), bf16[64,8,128]{2,1,0:T(8,128)(2,1)S(1)}, u32[]{:S(2)}, u32[]{:S(2)}) async-start(bf16[64,8,128]{2,1,0:T(8,128)(2,1)} %bitcast.17), calls=%async_computation.1 | async-start | bytes 262144 | tf_op jit(solution)/shard_map/all_to_all | solution.py:36
  64.3 0.8 copy-start.3
  65.1 2.1 %copy-start = (bf16[512,3072]{1,0:T(8,128)(2,1)S(1)}, bf16[512,3072]{1,0:T(8,128)(2,1)}, u32[]{:S(2)}) copy-start(bf16[512,3072]{1,0:T(8,128)(2,1)} %w_ref.1) | copy-start | bytes 9437188

commit v3 on v2

--- a/solution.py
+++ b/solution.py
@@ -10,31 +10,134 @@
 BLOCK = 384
 
 
+def exchange_kernel(
+    state_ref, total_ref, o_ref,
+    states, totals, row_state, row_total, rows_got, row_totals_got, back, mine,
+    state_send, state_recv, total_send, total_recv, row_send, row_recv,
+    row_total_send, row_total_recv, back_send, back_recv,
+):
+    me = lax.axis_index("seq")
+    near = lax.rem(me, 8)
+    far = lax.div(me, 8)
+    head = lax.div(near, 2)
+
+    def along(offset):
+        return far * 8 + lax.rem(near + offset, 8)
+
+    def across(offset):
+        return lax.rem(far + offset, 8) * 8 + near
+
+    barrier = pltpu.get_barrier_semaphore()
+    for offset in range(1, 8):
+        for peer in (along(offset), across(offset)):
+            pl.semaphore_signal(
+                barrier, inc=1, device_id={"seq": peer}, device_id_type=pl.DeviceIdType.MESH
+            )
+    pl.semaphore_wait(barrier, 14)
+
+    def send(source, target, send_sem, recv_sem, to):
+        copy = pltpu.make_async_remote_copy(
+            src_ref=source, dst_ref=target, send_sem=send_sem, recv_sem=recv_sem,
+            device_id={"seq": to}, device_id_type=pl.DeviceIdType.MESH,
+        )
+        copy.start()
+        return copy
+
+    order = (4, 3, 5, 2, 6, 1, 7)
+    first = []
+    for offset in order:
+        i = offset - 1
+        peer = lax.rem(near + offset, 8)
+        first.append(
+            send(total_ref, totals.at[near], total_send.at[i], total_recv.at[i], along(offset))
+        )
+        first.append(
+            send(
+                state_ref.at[peer], states.at[near],
+                state_send.at[i], state_recv.at[i], along(offset),
+            )
+        )
+    totals[near] = total_ref[...]
+    states[near] = state_ref[near]
+    for copy in first:
+        copy.wait_recv()
+    decays = []
+    pieces = []
+    total = jnp.zeros(total_ref.shape, jnp.float32)
+    running = jnp.zeros(o_ref.shape[1:], jnp.float32)
+    for z in range(8):
+        decay = jnp.exp(totals[z, pl.ds(head, 1), :])
+        piece = states[z].astype(jnp.float32)
+        running = decay * running + piece
+        total = total + totals[z]
+        decays.append(decay)
+        pieces.append(piece)
+    row_state[...] = running.astype(jnp.bfloat16)
+    row_total[...] = total
+    second = []
+    for offset in order:
+        i = offset - 1
+        second.append(
+            send(
+                row_total, row_totals_got.at[far],
+                row_total_send.at[i], row_total_recv.at[i], across(offset),
+            )
+        )
+        second.append(
+            send(row_state, rows_got.at[far], row_send.at[i], row_recv.at[i], across(offset))
+        )
+    rows_got[far] = row_state[...]
+    row_totals_got[far] = row_total[...]
+    for copy in second:
+        copy.wait_recv()
+    running = jnp.zeros(o_ref.shape[1:], jnp.float32)
+    for y in range(8):
+        decay = jnp.exp(row_totals_got[y, pl.ds(head, 1), :])
+        moved = decay * running + rows_got[y].astype(jnp.float32)
+        running = jnp.where(y < far, moved, running)
+    for z in range(8):
+        back[z] = running.astype(jnp.bfloat16)
+        running = decays[z] * running + pieces[z]
+    third = []
+    for offset in order:
+        i = offset - 1
+        peer = lax.rem(near + offset, 8)
+        third.append(
+            send(back.at[peer], mine.at[near], back_send.at[i], back_recv.at[i], along(offset))
+        )
+    mine[near] = back[near]
+    for copy in third:
+        copy.wait_recv()
+    o_ref[...] = mine[...].astype(jnp.float32)
+    for copy in first + second + third:
+        copy.wait_send()
+
+
 def exchange(running, decay_sum):
     head_count = running.shape[0]
-    ways = lax.axis_size("seq")
-    per_head = ways // head_count
-    rows = HEAD // per_head
-    pieces = running.astype(jnp.bfloat16).reshape(ways, rows, HEAD)
-    high = lax.reduce_precision(decay_sum, 8, 7)
-    middle = lax.reduce_precision(decay_sum - high, 8, 7)
-    low = lax.reduce_precision(decay_sum - high - middle, 8, 7)
-    parts = jnp.stack([high, middle, low] + [jnp.zeros_like(high)] * (rows - 3), axis=1)
-    parts = jnp.repeat(parts.astype(jnp.bfloat16), per_head, axis=0)
-    parts = jnp.broadcast_to(parts[:, :, None], (ways, rows, HEAD))
-    sent = jnp.concatenate([pieces, parts], axis=1)
-    got = lax.all_to_all(sent, "seq", 0, 0, tiled=True).astype(jnp.float32)
-    states = got[:, :rows].reshape(ways, rows * HEAD)
-    totals = jnp.sum(got[:, rows : rows + 3, 0], axis=1)
-    place = jnp.arange(ways)
-    target, origin, between = place[None, :, None], place[None, None, :], place[:, None, None]
-    inside = (between > origin) & (between < target)
-    spans = jnp.sum(jnp.where(inside, totals[:, None, None], 0.0), axis=0)
-    factors = jnp.where(place[None, :] < place[:, None], jnp.exp(spans), 0.0)
-    starts = jnp.dot(factors, states, precision=lax.Precision.HIGHEST)
-    back = starts.astype(jnp.bfloat16).reshape(ways, rows, HEAD)
-    mine = lax.all_to_all(back, "seq", 0, 0, tiled=True)
-    return mine.astype(jnp.float32).reshape(head_count, HEAD, HEAD)
+    rows = head_count * HEAD // 8
+    pieces = running.astype(jnp.bfloat16).reshape(8, rows, HEAD)
+    totals = jnp.pad(
+        jnp.broadcast_to(decay_sum[:, None], (head_count, HEAD)), ((0, 8 - head_count), (0, 0))
+    )
+    seven = pltpu.SemaphoreType.DMA((7,))
+    vmem = pl.BlockSpec(memory_space=pltpu.VMEM)
+    block = pltpu.VMEM((8, rows, HEAD), jnp.bfloat16)
+    sums = pltpu.VMEM((8, 8, HEAD), jnp.float32)
+    incoming = pl.pallas_call(
+        exchange_kernel,
+        out_shape=jax.ShapeDtypeStruct((8, rows, HEAD), jnp.float32),
+        in_specs=[vmem] * 2,
+        out_specs=vmem,
+        scratch_shapes=[
+            block, sums,
+            pltpu.VMEM((rows, HEAD), jnp.bfloat16),
+            pltpu.VMEM((8, HEAD), jnp.float32),
+            block, sums, block, block,
+        ] + [seven] * 10,
+        compiler_params=pltpu.CompilerParams(collective_id=1, has_side_effects=True),
+    )(pieces, totals)
+    return incoming.reshape(head_count, HEAD, HEAD)
 
 
 def project_kernel(

time: 99.3 us -> 84.5 us (0.85)
  Pallas kernels: 30.9 us -> 61.2 us
  starting transfers between devices: 23.2 us -> 0 us
  waiting for transfers between devices: 19.2 us -> 0 us
  matrix products: 9.92 us -> 8.53 us
    pallas_call x0 -> x1, Pallas kernels: none -> 30.4 us  [exchange(): pl.pallas_call(exchange_kernel, out_shape=jax.ShapeDtypeStruct((8, rows,...]
    all_to_all x2 -> x0, starting transfers between devices: 23.2 us -> none  [the longest x1 17.1 us: exchange(): got = lax.all_to_all(sent, 'seq', 0, 0, tiled=True).astype(jnp.float32)]
    all_to_all x2 -> x0, waiting for transfers between devices: 19.2 us -> none  [the longest x1 12.3 us: exchange(): got = lax.all_to_all(sent, 'seq', 0, 0, tiled=True).astype(jnp.float32)]
    reduce_sum x2 -> x0, other arithmetic: 1.38 us -> none  [the longest x1 0.82 us: exchange(): spans = jnp.sum(jnp.where(inside, totals[:, None, None], 0.0), axis=0)]
    dot_general x1, matrix products: 1.5 us -> 0.37 us  [shards(): jnp.einsum('ntha,nthb->nhab', scaled_keys, value_blocks, preferred_elemen...]
    unnamed x11 -> x14, local copies, waits for them, and re-layouts: 1.89 us -> 2.09 us
    another operation x6 -> x3, other arithmetic: 2.53 us -> 2.49 us
  transfers between devices with their start and end apart: 2 -> 0, of which waited for: 2 -> 0; matrix products, arithmetic and copies ran while one was open for 5% -> 0% of each run, Pallas kernels for 0% -> 0%
where the time goes in v3:
time: 84.5 us; the launch traced here: 84.2 us
  Pallas kernels  61.2 us (72%)
  matrix products  8.53 us (10%)
  local copies, waits for them, and re-layouts  8.01 us (9%)
  other arithmetic  6.21 us (7%)
    pallas_call x1, Pallas kernels, project(): pl.pallas_call(project_kernel, out_shape=jax.ShapeDtypeStruct((tokens, wi...  30.8 us
    pallas_call x1, Pallas kernels, exchange(): pl.pallas_call(exchange_kernel, out_shape=jax.ShapeDtypeStruct((8, rows,...  30.4 us
    dot_general x1, matrix products, shards(): jnp.einsum('hnts,nshb->nthb', weighted, value_blocks, preferred_element_t...  4.45 us
    dot_general x1, matrix products, shards(): jnp.einsum('ntha,nhab->nthb', scaled_queries, starts, precision=lax.Preci...  3.71 us
    another operation x3, other arithmetic  2.49 us
    reshape x2, local copies, waits for them, and re-layouts, shards(): key_blocks = key_rows.reshape(blocks, BLOCK, head_count, HEAD)  2.45 us
    unnamed x14, local copies, waits for them, and re-layouts  2.09 us
    convert_element_type x1, other arithmetic, shards(): attended = (attention * norm_gain * gates).astype(jnp.bfloat16)  1.75 us

profile of v3, /device:TPU:1, one launch (start us, length us, event | category | flops | bytes accessed | tf_op | source)
XLA Modules:
  0.0 84.2 jit_solution(769835591075595776)
XLA Ops:
  0.0 0.7 copy.22
  0.7 2.4 %reduce-window.6 = f32[4,2,3,128]{3,2,1,0:T(4,128)S(1)} reduce-window(f32[4,2,3,128]{3,2,1,0:T(4,128)S(1)} %copy.22, f32[]{:T(128)} %constant.4.clone.1), window={size=1x1x1x128 pad=0_0x0_0x0_0x127_0}, to_apply=%region_0.0 | reduce-window | flops 390144 | bytes 24580 | tf_op jit(solution)/shard_map/reduce-window
  3.1 0.1 slice.30
  3.2 0.1 copy.23
  3.3 0.1 copy.24
  3.4 0.1 broadcast_add_fusion
  3.5 0.1 slice.32
  3.6 0.1 copy.28
  3.7 0.1 copy.30
  3.8 0.1 exponential_bitcast_fusion.1
  3.9 0.0 copy-start.2
  3.9 1.8 %reshape.82 = bf16[2,384,4,128]{3,2,1,0:T(4,128)(2,1)S(1)} reshape(bf16[768,512]{1,0:T(8,128)(2,1)} %param.8) | data formatting | bytes 1572864 | tf_op jit(solution)/shard_map/reshape | solution.py:316
  5.8 0.6 copy.29
  6.4 0.0 copy-done.2
  6.4 0.2 reshape.85
  6.6 0.0 copy-start.4
  6.6 0.9 %copy-done.4 = bf16[2,384,4,128]{3,2,1,0:T(4,128)(2,1)} copy-done((bf16[2,384,4,128]{3,2,1,0:T(4,128)(2,1)}, bf16[2,384,4,128]{3,2,1,0:T(4,128)(2,1)S(1)}, u32[]{:S(2)}) %copy-start.4) | copy-done | bytes 786456
  7.5 0.4 fusion.14
  7.9 0.0 copy-start.3
  7.9 0.1 mul.78
  8.0 0.1 mul.79
  8.1 0.1 mul.82
  8.2 0.1 mul.83
  8.3 0.8 add_convert_fusion.state_ref
  9.0 0.7 pad.7.total_ref
  9.7 30.4 %shard_map.73 = f32[8,64,128]{2,1,0:T(8,128)} custom-call(bf16[8,64,128]{2,1,0:T(8,128)(2,1)} %add_convert_fusion.state_ref, f32[8,128]{1,0:T(8,128)} %pad.7.total_ref), custom_call_target="tpu_custom_call" | custom-call | tf_op jit(solution)/shard_map/pallas_call | solution.py:127
  40.1 1.1 %add_add_fusion = f32[1,4,128,128]{3,2,1,0:T(8,128)S(1)} fusion(f32[1,4,128,128]{3,2,1,0:T(8,128)} %bitcast.38, f32[4]{0:T(128)S(1)} %broadcast_multiply_fusion, f32[4]{0:T(128)S(1)} %get-tuple-element.9, f32[2,4,128,128]{3,2,1,0:T(8,128)S(1)} %fusion.14), kind=kLoop, calls=%fused_computation.27 | loop fusion | flops 196608 | bytes 786464 | tf_op jit(solution)/shard_map/add | solution.py:347
  41.2 0.0 copy-done.3
  41.2 0.2 reshape.81
  41.5 0.0 copy-start.1
  41.5 4.4 %fusion = f32[2,4,384,128]{2,3,1,0:T(8,128)} fusion(f32[4,2,384]{2,0,1:T(4,128)S(1)} %copy.25, pred[384,384]{1,0:T(8,128)(4,1)S(1)} %iota_compare_fusion, bf16[2,384,4,128]{1,3,2,0:T(8,128)(2,1)S(1)} %copy.29, bf16[2,384,4,128]{3,2,1,0:T(4,128)(2,1)S(1)} %reshape.81, bf16[2,384,4,128]{3,2,1,0:T(4,128)(2,1)} %copy-done.4), kind=kOutput, calls=%fused_computation.1 | convolution fusion | flops 609878016 | bytes 4091904 | tf_op jit(solution)/shard_map/hnts,nshb->nthb/dot_general | solution.py:327
  45.9 0.0 copy-done.1
  45.9 3.7 %multiply_reduce_fusion = (f32[2,384]{1,0:T(2,128)S(1)}, f32[2,384,4,128]{1,3,2,0:T(8,128)S(1)}) fusion(f32[2,384,4]{1,2,0:T(4,128)S(1)} %copy.34, bf16[2,384,4,128]{3,2,1,0:T(4,128)(2,1)S(1)} %reshape.81, f32[1,4,128,128]{3,2,1,0:T(8,128)S(1)} %add_add_fusion, f32[1,4,128,128]{3,2,1,0:T(8,128)S(1)} %bitcast.39, f32[2,4,384,128]{2,3,1,0:T(8,128)} %fusion), kind=kOutput, calls=%fused_computation.11 | convolution fusion | flops 606076160 | bytes 4471808 | tf_op jit(solution)/shard_map/ntha,nhab->nthb/dot_general | solution.py:353
  49.6 0.0 copy-start.5
  49.6 0.8 copy.36
  50.4 0.0 copy-done.5
  50.4 0.0 copy-start
  50.4 1.7 %fusion.8.a_ref = bf16[768,512]{1,0:T(8,128)(2,1)S(1)} fusion(f32[96,8,4,128]{3,2,1,0:T(4,128)S(1)} %bitcast.37, bf16[768,512]{1,0:T(8,128)(2,1)} %param.11, f32[512]{0:T(512)S(1)} %copy-done.5), kind=kLoop, calls=%fused_computation.9 | loop fusion | flops 2752512 | bytes 3147776 | tf_op jit(solution)/shard_map/convert_element_type | solution.py:357
  52.2 0.4 copy-done
  52.6 30.8 %shard_map.74 = bf16[768,384]{1,0:T(8,128)(2,1)S(1)} custom-call(bf16[768,512]{1,0:T(8,128)(2,1)S(1)} %fusion.8.a_ref, bf16[512,3072]{1,0:T(8,128)(2,1)S(1)} %copy-done, f32[1,768]{1,0:T(1,128)S(1)} %bitcast.36), custom_call_target="tpu_custom_call" | custom-call | tf_op jit(solution)/shard_map/pallas_call | solution.py:289
  83.4 0.8 copy.55
  (12 shorter events, 0.1 us)
Async XLA Ops:
  3.9 2.5 %copy-start.2 = (bf16[768,512]{1,0:T(8,128)(2,1)S(1)}, bf16[768,512]{1,0:T(8,128)(2,1)}, u32[]{:S(2)}) copy-start(bf16[768,512]{1,0:T(8,128)(2,1)} %param.9) | copy-start | bytes 2359300
  6.6 0.9 %copy-start.4 = (bf16[2,384,4,128]{3,2,1,0:T(4,128)(2,1)}, bf16[2,384,4,128]{3,2,1,0:T(4,128)(2,1)S(1)}, u32[]{:S(2)}) copy-start(bf16[2,384,4,128]{3,2,1,0:T(4,128)(2,1)S(1)} %reshape.85) | copy-start | bytes 2359300
  7.9 33.3 %copy-start.3 = (bf16[768,512]{1,0:T(8,128)(2,1)S(1)}, bf16[768,512]{1,0:T(8,128)(2,1)}, u32[]{:S(2)}) copy-start(bf16[768,512]{1,0:T(8,128)(2,1)} %param.7) | copy-start | bytes 2359300
  41.5 4.5 %copy-start.1 = (f32[8,64,128]{2,1,0:T(8,128)S(1)}, f32[8,64,128]{2,1,0:T(8,128)}, u32[]{:S(2)}) copy-start(f32[8,64,128]{2,1,0:T(8,128)} %shard_map.73) | copy-start | bytes 786436
  49.6 0.8 copy-start.5
  50.4 2.1 %copy-start = (bf16[512,3072]{1,0:T(8,128)(2,1)S(1)}, bf16[512,3072]{1,0:T(8,128)(2,1)}, u32[]{:S(2)}) copy-start(bf16[512,3072]{1,0:T(8,128)(2,1)} %w_ref.1) | copy-start | bytes 9437188

commit v4 on v3

--- a/solution.py
+++ b/solution.py
@@ -11,8 +11,9 @@
 
 
 def exchange_kernel(
-    state_ref, total_ref, o_ref,
-    states, totals, row_state, row_total, rows_got, row_totals_got, back, mine,
+    state_ref, total_ref, first_total_ref, first_state_ref, cumulative_ref,
+    q_ref, k_ref, v_ref, gate_ref, gain_ref, o_ref, sq_ref,
+    attention, states, totals, row_state, row_total, rows_got, row_totals_got, back, mine,
     state_send, state_recv, total_send, total_recv, row_send, row_recv,
     row_total_send, row_total_recv, back_send, back_recv,
 ):
@@ -59,12 +60,34 @@
         )
     totals[near] = total_ref[...]
     states[near] = state_ref[near]
+    by_token = jnp.transpose(cumulative_ref[...])
+    causal = lax.broadcasted_iota(jnp.int32, (BLOCK, BLOCK), 0) >= lax.broadcasted_iota(
+        jnp.int32, (BLOCK, BLOCK), 1
+    )
+
+    def inside(h):
+        columns = slice(h * HEAD, (h + 1) * HEAD)
+        for block in range(2):
+            rows = slice(block * BLOCK, (block + 1) * BLOCK)
+            scores = lax.dot_general(
+                q_ref[rows, columns], k_ref[rows, columns], (((1,), (1,)), ((), ())),
+                preferred_element_type=jnp.float32,
+            )
+            spread = by_token[rows, h : h + 1] - cumulative_ref[h : h + 1, rows]
+            decay = jnp.where(causal, jnp.exp(jnp.where(causal, spread, 0.0)), 0.0)
+            attention[rows, columns] = jnp.dot(
+                (scores * decay).astype(jnp.bfloat16), v_ref[rows, columns],
+                preferred_element_type=jnp.float32,
+            )
+
+    inside(0)
+    inside(1)
     for copy in first:
         copy.wait_recv()
     decays = []
     pieces = []
     total = jnp.zeros(total_ref.shape, jnp.float32)
-    running = jnp.zeros(o_ref.shape[1:], jnp.float32)
+    running = jnp.zeros(row_state.shape, jnp.float32)
     for z in range(8):
         decay = jnp.exp(totals[z, pl.ds(head, 1), :])
         piece = states[z].astype(jnp.float32)
@@ -88,9 +111,10 @@
         )
     rows_got[far] = row_state[...]
     row_totals_got[far] = row_total[...]
+    inside(2)
     for copy in second:
         copy.wait_recv()
-    running = jnp.zeros(o_ref.shape[1:], jnp.float32)
+    running = jnp.zeros(row_state.shape, jnp.float32)
     for y in range(8):
         decay = jnp.exp(row_totals_got[y, pl.ds(head, 1), :])
         moved = decay * running + rows_got[y].astype(jnp.float32)
@@ -106,38 +130,71 @@
             send(back.at[peer], mine.at[near], back_send.at[i], back_recv.at[i], along(offset))
         )
     mine[near] = back[near]
+    inside(3)
     for copy in third:
         copy.wait_recv()
-    o_ref[...] = mine[...].astype(jnp.float32)
+    squares = [jnp.zeros((BLOCK, 1), jnp.float32) for block in range(2)]
+    for h in range(HEADS // 8):
+        columns = slice(h * HEAD, (h + 1) * HEAD)
+        start = mine[2 * h : 2 * h + 2].astype(jnp.float32).reshape(HEAD, HEAD)
+        for block in range(2):
+            rows = slice(block * BLOCK, (block + 1) * BLOCK)
+            if block == 1:
+                start = jnp.exp(first_total_ref[h : h + 1, :]) * start + first_state_ref[h]
+            query = q_ref[rows, columns].astype(jnp.float32) * jnp.exp(by_token[rows, h : h + 1])
+            full = attention[rows, columns] + jnp.dot(
+                query, start, precision=lax.Precision.HIGHEST,
+                preferred_element_type=jnp.float32,
+            )
+            squares[block] = squares[block] + jnp.sum(full * full, axis=1, keepdims=True)
+            gates = jax.nn.sigmoid(gate_ref[rows, columns].astype(jnp.float32))
+            o_ref[rows, columns] = (full * gain_ref[:, columns] * gates).astype(jnp.bfloat16)
+    for block in range(2):
+        spread = jnp.broadcast_to(squares[block], (BLOCK, HEAD))
+        sq_ref[:, block * BLOCK : (block + 1) * BLOCK] = jnp.transpose(spread)[:1]
     for copy in first + second + third:
         copy.wait_send()
 
 
-def exchange(running, decay_sum):
+def exchange(
+    running, decay_sum, first_total, first_state, cumulative,
+    queries, key_rows, value_rows, gate_logits, norm_gain,
+):
     head_count = running.shape[0]
     rows = head_count * HEAD // 8
     pieces = running.astype(jnp.bfloat16).reshape(8, rows, HEAD)
-    totals = jnp.pad(
-        jnp.broadcast_to(decay_sum[:, None], (head_count, HEAD)), ((0, 8 - head_count), (0, 0))
-    )
+
+    def spread_out(total):
+        return jnp.pad(
+            jnp.broadcast_to(total[:, None], (head_count, HEAD)), ((0, 8 - head_count), (0, 0))
+        )
+
+    tokens, columns = queries.shape
+    cumulative = jnp.pad(cumulative.reshape(head_count, tokens), ((0, 8 - head_count), (0, 0)))
     seven = pltpu.SemaphoreType.DMA((7,))
     vmem = pl.BlockSpec(memory_space=pltpu.VMEM)
     block = pltpu.VMEM((8, rows, HEAD), jnp.bfloat16)
     sums = pltpu.VMEM((8, 8, HEAD), jnp.float32)
-    incoming = pl.pallas_call(
+    return pl.pallas_call(
         exchange_kernel,
-        out_shape=jax.ShapeDtypeStruct((8, rows, HEAD), jnp.float32),
-        in_specs=[vmem] * 2,
-        out_specs=vmem,
+        out_shape=[
+            jax.ShapeDtypeStruct((tokens, columns), jnp.bfloat16),
+            jax.ShapeDtypeStruct((1, tokens), jnp.float32),
+        ],
+        in_specs=[vmem] * 10,
+        out_specs=[vmem] * 2,
         scratch_shapes=[
+            pltpu.VMEM((tokens, columns), jnp.float32),
             block, sums,
             pltpu.VMEM((rows, HEAD), jnp.bfloat16),
             pltpu.VMEM((8, HEAD), jnp.float32),
             block, sums, block, block,
         ] + [seven] * 10,
         compiler_params=pltpu.CompilerParams(collective_id=1, has_side_effects=True),
-    )(pieces, totals)
-    return incoming.reshape(head_count, HEAD, HEAD)
+    )(
+        pieces, spread_out(decay_sum), spread_out(first_total), first_state, cumulative,
+        queries, key_rows, value_rows, gate_logits, norm_gain[None, :],
+    )
 
 
 def project_kernel(
@@ -312,21 +369,10 @@
     columns = queries.shape[1]
     head_count = columns // HEAD
     blocks = rows_here // BLOCK
-    query_blocks = queries.reshape(blocks, BLOCK, head_count, HEAD)
     key_blocks = key_rows.reshape(blocks, BLOCK, head_count, HEAD)
     value_blocks = value_rows.reshape(blocks, BLOCK, head_count, HEAD)
     cumulative = jnp.cumsum(log_decay.reshape(head_count, blocks, BLOCK), axis=2)
     totals = cumulative[:, :, -1]
-    causal = jnp.tril(jnp.ones((BLOCK, BLOCK), dtype=jnp.bool_))
-    spread = cumulative[:, :, :, None] - cumulative[:, :, None, :]
-    decays = jnp.where(causal, jnp.exp(jnp.where(causal, spread, 0.0)), 0.0)
-    scores = jnp.einsum(
-        "ntha,nsha->hnts", query_blocks, key_blocks, preferred_element_type=jnp.float32
-    )
-    weighted = (scores * decays).astype(jnp.bfloat16)
-    inside = jnp.einsum(
-        "hnts,nshb->nthb", weighted, value_blocks, preferred_element_type=jnp.float32
-    )
     key_scale = jnp.exp(totals[:, :, None] - cumulative).transpose(1, 2, 0)[..., None]
     scaled_keys = (key_blocks.astype(jnp.float32) * key_scale).astype(jnp.bfloat16)
     block_states = jnp.einsum(
@@ -334,28 +380,14 @@
     )
     running = jnp.zeros((head_count, HEAD, HEAD), jnp.float32)
     decay_sum = jnp.zeros((head_count,), jnp.float32)
-    local_before = []
-    decay_before = []
     for block in range(blocks):
-        local_before.append(running)
-        decay_before.append(decay_sum)
         running = jnp.exp(totals[:, block])[:, None, None] * running + block_states[block]
         decay_sum = decay_sum + totals[:, block]
-    incoming = exchange(running, decay_sum)
-    starts = jnp.stack(
-        [
-            jnp.exp(decay_before[block])[:, None, None] * incoming + local_before[block]
-            for block in range(blocks)
-        ]
-    )
-    query_scale = jnp.exp(cumulative).transpose(1, 2, 0)[..., None]
-    scaled_queries = query_blocks.astype(jnp.float32) * query_scale
-    carried = jnp.einsum("ntha,nhab->nthb", scaled_queries, starts, precision=lax.Precision.HIGHEST)
-    attention = (inside + carried).reshape(rows_here, columns)
-    squares = jnp.sum(attention * attention, axis=1)
-    gates = jax.nn.sigmoid(gate_logits.astype(jnp.float32))
-    attended = (attention * norm_gain * gates).astype(jnp.bfloat16)
-    return project(attended, out_weight, squares[None, :])
+    attended, squares = exchange(
+        running, decay_sum, totals[:, 0], block_states[0], cumulative,
+        queries, key_rows, value_rows, gate_logits, norm_gain,
+    )
+    return project(attended, out_weight, squares)
 
 
 def solution(mesh):

time: 84.5 us -> 79.2 us (0.937)
  matrix products: 8.53 us -> 0.36 us
  Pallas kernels: 61.2 us -> 64.6 us
  other arithmetic: 6.21 us -> 3.39 us
  local copies, waits for them, and re-layouts: 8.01 us -> 10.5 us
    dot_general x2 -> x0, matrix products: 8.16 us -> none  [the longest x1 4.45 us: shards(): jnp.einsum('hnts,nshb->nthb', weighted, value_blocks, preferred_element_t...]
    pallas_call x1, Pallas kernels: 30.4 us -> 33.8 us  [exchange(): pl.pallas_call(exchange_kernel, out_shape=[jax.ShapeDtypeStruct((tokens,...]
    reshape x4 -> x1, local copies, waits for them, and re-layouts: 3.34 us -> 0.01 us  [the longest x2 2.45 us: shards(): key_blocks = key_rows.reshape(blocks, BLOCK, head_count, HEAD)]
    convert_element_type x0 -> x2, local copies, waits for them, and re-layouts: none -> 2.43 us  [shards(): key_blocks.astype(jnp.float32) * key_scale]
    convert_element_type x1 -> x0, other arithmetic: 1.75 us -> none  [shards(): attended = (attention * norm_gain * gates).astype(jnp.bfloat16)]
    reshape x1, local copies, waits for them, and re-layouts: 0.18 us -> 1.75 us  [shards(): value_blocks = value_rows.reshape(blocks, BLOCK, head_count, HEAD)]
    pad x2 -> x5, local copies, waits for them, and re-layouts: 0.66 us -> 1.93 us  [the longest x4 1.33 us: spread_out(): jnp.pad(jnp.broadcast_to(total[:, None], (head_count, HEAD)), ((0, 8 - he...]
    add x1 -> x0, other arithmetic: 1.05 us -> none  [shards(): jnp.exp(decay_before[block])[:, None, None] * incoming + local_before[block]]
where the time goes in v4:
time: 79.2 us; the launch traced here: 79 us
  Pallas kernels  64.6 us (82%)
  local copies, waits for them, and re-layouts  10.5 us (13%)
  other arithmetic  3.39 us (4%)
    pallas_call x1, Pallas kernels, exchange(): pl.pallas_call(exchange_kernel, out_shape=[jax.ShapeDtypeStruct((tokens,...  33.8 us
    pallas_call x1, Pallas kernels, project(): pl.pallas_call(project_kernel, out_shape=jax.ShapeDtypeStruct((tokens, wi...  30.8 us
    unnamed x9, local copies, waits for them, and re-layouts  2.64 us
    another operation x3, other arithmetic  2.52 us
    convert_element_type x2, local copies, waits for them, and re-layouts, shards(): key_blocks.astype(jnp.float32) * key_scale  2.43 us
    reshape x1, local copies, waits for them, and re-layouts, shards(): value_blocks = value_rows.reshape(blocks, BLOCK, head_count, HEAD)  1.75 us

profile of v4, /device:TPU:1, one launch (start us, length us, event | category | flops | bytes accessed | tf_op | source)
XLA Modules:
  0.0 79.0 jit_solution(12125592869603087284)
XLA Ops:
  0.0 1.7 %reshape.43 = f32[2,384,4,128]{3,2,1,0:T(4,128)S(1)} reshape(bf16[768,512]{1,0:T(8,128)(2,1)} %k_ref.1) | data formatting | bytes 2359296 | tf_op jit(solution)/shard_map/convert_element_type | solution.py:377
  1.8 0.7 copy.21
  2.4 0.0 copy-start.3
  2.5 1.8 %reshape.42 = bf16[2,384,4,128]{3,2,1,0:T(4,128)(2,1)S(1)} reshape(bf16[768,512]{1,0:T(8,128)(2,1)} %v_ref.1) | data formatting | bytes 1572864 | tf_op jit(solution)/shard_map/reshape | solution.py:373
  4.2 0.0 copy-done.3
  4.2 2.4 %reduce-window.6 = f32[4,2,3,128]{3,2,1,0:T(4,128)S(1)} reduce-window(f32[4,2,3,128]{3,2,1,0:T(4,128)S(1)} %copy.15, f32[]{:T(128)} %constant.6.clone.1), window={size=1x1x1x128 pad=0_0x0_0x0_0x127_0}, to_apply=%region_0.0 | reduce-window | flops 390144 | bytes 24580 | tf_op jit(solution)/shard_map/reduce-window
  6.7 0.1 slice.32
  6.8 0.1 copy.16
  6.9 0.1 copy.17
  7.0 0.1 broadcast_add_fusion
  7.1 0.1 slice.34
  7.2 0.1 copy.18
  7.3 0.1 copy.19
  7.4 0.1 exponential_bitcast_fusion
  7.5 0.4 fusion
  7.8 0.8 slice_bitcast_fusion.1
  8.6 0.1 mul.38
  8.7 0.1 mul.39
  8.8 0.1 mul.34
  8.9 0.1 mul.35
  9.0 0.8 add_convert_fusion.state_ref
  9.7 0.7 pad.16.total_ref
  10.4 0.7 pad.18.first_total_ref
  11.1 0.6 pad.19.cumulative_ref
  11.7 0.0 copy-start
  11.7 33.8 %shard_map.73 = (bf16[768,512]{1,0:T(8,128)(2,1)}, f32[1,768]{1,0:T(1,128)}) custom-call(bf16[8,64,128]{2,1,0:T(8,128)(2,1)} %add_convert_fusion.state_ref, f32[8,128]{1,0:T(8,128)} %pad.16.total_ref, f32[8,128]{1,0:T(8,128)} %pad.18.first_total_ref, f32[4,128,128]{2,1,0:T(8,128)} %get-tuple-element.9.first_state_ref, f32[8,768]{1,0:T(8,128)} %pad.19.cumulative_ref, ...), custom_call_target="tpu_custom_call" | custom-call | tf_op jit(solution)/shard_map/pallas_call | solution.py:178
  45.5 0.0 copy-done
  45.5 0.0 copy-start.1
  45.5 1.1 %copy-done.1 = bf16[768,512]{1,0:T(8,128)(2,1)S(1)} copy-done((bf16[768,512]{1,0:T(8,128)(2,1)S(1)}, bf16[768,512]{1,0:T(8,128)(2,1)}, u32[]{:S(2)}) %copy-start.1) | copy-done | bytes 786456
  46.6 0.0 copy-start.2
  46.6 0.7 copy-done.2
  47.3 30.8 %shard_map.74 = bf16[768,384]{1,0:T(8,128)(2,1)S(1)} custom-call(bf16[768,512]{1,0:T(8,128)(2,1)S(1)} %copy-done.1, bf16[512,3072]{1,0:T(8,128)(2,1)S(1)} %copy-done, f32[1,768]{1,0:T(1,128)S(1)} %copy-done.2), custom_call_target="tpu_custom_call" | custom-call | tf_op jit(solution)/shard_map/pallas_call | solution.py:346
  78.1 0.8 %copy.26 = bf16[768,384]{1,0:T(8,128)(2,1)} copy(bf16[768,384]{1,0:T(8,128)(2,1)S(1)} %shard_map.74) | data formatting | bytes 1179648
  (10 shorter events, 0.1 us)
Async XLA Ops:
  2.4 1.8 %copy-start.3 = (f32[4,768]{1,0:T(4,128)S(1)}, f32[4,768]{1,0:T(4,128)}, u32[]{:S(2)}) copy-start(f32[4,768]{1,0:T(4,128)} %param.10) | copy-start | bytes 36868
  11.7 33.8 %copy-start = (bf16[512,3072]{1,0:T(8,128)(2,1)S(1)}, bf16[512,3072]{1,0:T(8,128)(2,1)}, u32[]{:S(2)}) copy-start(bf16[512,3072]{1,0:T(8,128)(2,1)} %w_ref.1) | copy-start | bytes 9437188
  45.5 1.1 %copy-start.1 = (bf16[768,512]{1,0:T(8,128)(2,1)S(1)}, bf16[768,512]{1,0:T(8,128)(2,1)}, u32[]{:S(2)}) copy-start(bf16[768,512]{1,0:T(8,128)(2,1)} %get-tuple-element.7.a_ref) | copy-start | bytes 2359300
  46.6 0.7 copy-start.2

commit v5 on v4

--- a/solution.py
+++ b/solution.py
@@ -11,9 +11,8 @@
 
 
 def exchange_kernel(
-    state_ref, total_ref, first_total_ref, first_state_ref, cumulative_ref,
-    q_ref, k_ref, v_ref, gate_ref, gain_ref, o_ref, sq_ref,
-    attention, states, totals, row_state, row_total, rows_got, row_totals_got, back, mine,
+    decay_ref, q_ref, k_ref, v_ref, gate_ref, gain_ref, o_ref, sq_ref,
+    state_ref, total_ref, first_total_ref, first_state_ref, cumulative_ref, attention, states, totals, row_state, row_total, rows_got, row_totals_got, back, mine,
     state_send, state_recv, total_send, total_recv, row_send, row_recv,
     row_total_send, row_total_recv, back_send, back_recv,
 ):
@@ -34,6 +33,44 @@
             pl.semaphore_signal(
                 barrier, inc=1, device_id={"seq": peer}, device_id_type=pl.DeviceIdType.MESH
             )
+    row_index = lax.broadcasted_iota(jnp.int32, (BLOCK, BLOCK), 0)
+    column_index = lax.broadcasted_iota(jnp.int32, (BLOCK, BLOCK), 1)
+    causal = row_index >= column_index
+    upto = jnp.where(row_index <= column_index, 1.0, 0.0).astype(jnp.float32)
+    heads = HEADS // 8
+    cumulative_ref[...] = jnp.zeros(cumulative_ref.shape, jnp.float32)
+    for block in range(2):
+        rows = slice(block * BLOCK, (block + 1) * BLOCK)
+        cumulative_ref[:heads, rows] = jnp.dot(
+            decay_ref[:, rows], upto, precision=lax.Precision.HIGHEST,
+            preferred_element_type=jnp.float32,
+        )
+    by_token = jnp.transpose(cumulative_ref[...])
+    ends = [
+        jnp.broadcast_to(
+            cumulative_ref[:, (block + 1) * BLOCK - 1 : (block + 1) * BLOCK], total_ref.shape
+        )
+        for block in range(2)
+    ]
+    first_total_ref[...] = ends[0]
+    total_ref[...] = ends[0] + ends[1]
+    for h in range(heads):
+        columns = slice(h * HEAD, (h + 1) * HEAD)
+        sums = []
+        for block in range(2):
+            rows = slice(block * BLOCK, (block + 1) * BLOCK)
+            scale = jnp.exp(ends[block][h : h + 1, :] - by_token[rows, h : h + 1])
+            scaled = (k_ref[rows, columns].astype(jnp.float32) * scale).astype(jnp.bfloat16)
+            sums.append(
+                lax.dot_general(
+                    scaled, v_ref[rows, columns], (((0,), (0,)), ((), ())),
+                    preferred_element_type=jnp.float32,
+                )
+            )
+        first_state_ref[h] = sums[0]
+        whole = (jnp.exp(ends[1][h : h + 1, :]) * sums[0] + sums[1]).astype(jnp.bfloat16)
+        state_ref[2 * h] = whole[: HEAD // 2]
+        state_ref[2 * h + 1] = whole[HEAD // 2 :]
     pl.semaphore_wait(barrier, 14)
 
     def send(source, target, send_sem, recv_sem, to):
@@ -60,10 +97,6 @@
         )
     totals[near] = total_ref[...]
     states[near] = state_ref[near]
-    by_token = jnp.transpose(cumulative_ref[...])
-    causal = lax.broadcasted_iota(jnp.int32, (BLOCK, BLOCK), 0) >= lax.broadcasted_iota(
-        jnp.int32, (BLOCK, BLOCK), 1
-    )
 
     def inside(h):
         columns = slice(h * HEAD, (h + 1) * HEAD)
@@ -156,21 +189,9 @@
         copy.wait_send()
 
 
-def exchange(
-    running, decay_sum, first_total, first_state, cumulative,
-    queries, key_rows, value_rows, gate_logits, norm_gain,
-):
-    head_count = running.shape[0]
-    rows = head_count * HEAD // 8
-    pieces = running.astype(jnp.bfloat16).reshape(8, rows, HEAD)
-
-    def spread_out(total):
-        return jnp.pad(
-            jnp.broadcast_to(total[:, None], (head_count, HEAD)), ((0, 8 - head_count), (0, 0))
-        )
-
+def exchange(log_decay, queries, key_rows, value_rows, gate_logits, norm_gain):
     tokens, columns = queries.shape
-    cumulative = jnp.pad(cumulative.reshape(head_count, tokens), ((0, 8 - head_count), (0, 0)))
+    rows = columns // 8
     seven = pltpu.SemaphoreType.DMA((7,))
     vmem = pl.BlockSpec(memory_space=pltpu.VMEM)
     block = pltpu.VMEM((8, rows, HEAD), jnp.bfloat16)
@@ -181,9 +202,14 @@
             jax.ShapeDtypeStruct((tokens, columns), jnp.bfloat16),
             jax.ShapeDtypeStruct((1, tokens), jnp.float32),
         ],
-        in_specs=[vmem] * 10,
+        in_specs=[vmem] * 6,
         out_specs=[vmem] * 2,
         scratch_shapes=[
+            block,
+            pltpu.VMEM((8, HEAD), jnp.float32),
+            pltpu.VMEM((8, HEAD), jnp.float32),
+            pltpu.VMEM((columns // HEAD, HEAD, HEAD), jnp.float32),
+            pltpu.VMEM((8, tokens), jnp.float32),
             pltpu.VMEM((tokens, columns), jnp.float32),
             block, sums,
             pltpu.VMEM((rows, HEAD), jnp.bfloat16),
@@ -191,10 +217,7 @@
             block, sums, block, block,
         ] + [seven] * 10,
         compiler_params=pltpu.CompilerParams(collective_id=1, has_side_effects=True),
-    )(
-        pieces, spread_out(decay_sum), spread_out(first_total), first_state, cumulative,
-        queries, key_rows, value_rows, gate_logits, norm_gain[None, :],
-    )
+    )(log_decay, queries, key_rows, value_rows, gate_logits, norm_gain[None, :])
 
 
 def project_kernel(
@@ -365,27 +388,8 @@
 
 
 def shards(queries, key_rows, value_rows, log_decay, gate_logits, norm_gain, out_weight):
-    rows_here = queries.shape[0]
-    columns = queries.shape[1]
-    head_count = columns // HEAD
-    blocks = rows_here // BLOCK
-    key_blocks = key_rows.reshape(blocks, BLOCK, head_count, HEAD)
-    value_blocks = value_rows.reshape(blocks, BLOCK, head_count, HEAD)
-    cumulative = jnp.cumsum(log_decay.reshape(head_count, blocks, BLOCK), axis=2)
-    totals = cumulative[:, :, -1]
-    key_scale = jnp.exp(totals[:, :, None] - cumulative).transpose(1, 2, 0)[..., None]
-    scaled_keys = (key_blocks.astype(jnp.float32) * key_scale).astype(jnp.bfloat16)
-    block_states = jnp.einsum(
-        "ntha,nthb->nhab", scaled_keys, value_blocks, preferred_element_type=jnp.float32
-    )
-    running = jnp.zeros((head_count, HEAD, HEAD), jnp.float32)
-    decay_sum = jnp.zeros((head_count,), jnp.float32)
-    for block in range(blocks):
-        running = jnp.exp(totals[:, block])[:, None, None] * running + block_states[block]
-        decay_sum = decay_sum + totals[:, block]
     attended, squares = exchange(
-        running, decay_sum, totals[:, 0], block_states[0], cumulative,
-        queries, key_rows, value_rows, gate_logits, norm_gain,
+        log_decay, queries, key_rows, value_rows, gate_logits, norm_gain
     )
     return project(attended, out_weight, squares)
 

time: 79.2 us -> 67.2 us (0.85)
  local copies, waits for them, and re-layouts: 10.5 us -> 2.62 us
  other arithmetic: 3.39 us -> 0 us
    another operation x3 -> x0, other arithmetic: 2.52 us -> none
    convert_element_type x2 -> x0, local copies, waits for them, and re-layouts: 2.43 us -> none  [shards(): key_blocks.astype(jnp.float32) * key_scale]
    pad x5 -> x0, local copies, waits for them, and re-layouts: 1.93 us -> none  [the longest x4 1.33 us: spread_out(): jnp.pad(jnp.broadcast_to(total[:, None], (head_count, HEAD)), ((0, 8 - he...]
    reshape x2 -> x0, local copies, waits for them, and re-layouts: 1.76 us -> none  [the longest x1 1.75 us: shards(): value_blocks = value_rows.reshape(blocks, BLOCK, head_count, HEAD)]
    squeeze x2 -> x0, local copies, waits for them, and re-layouts: 0.87 us -> none  [the longest x1 0.77 us: shards(): block_states[block]]
    unnamed x9 -> x7, local copies, waits for them, and re-layouts: 2.64 us -> 2.62 us
where the time goes in v5:
time: 67.2 us; the launch traced here: 67 us
  Pallas kernels  64.4 us (96%)
  local copies, waits for them, and re-layouts  2.62 us (4%)
    pallas_call x1, Pallas kernels, exchange(): pl.pallas_call(exchange_kernel, out_shape=[jax.ShapeDtypeStruct((tokens,...  33.4 us
    pallas_call x1, Pallas kernels, project(): pl.pallas_call(project_kernel, out_shape=jax.ShapeDtypeStruct((tokens, wi...  31 us
    unnamed x7, local copies, waits for them, and re-layouts  2.62 us

profile of v5, /device:TPU:1, one launch (start us, length us, event | category | flops | bytes accessed | tf_op | source)
XLA Modules:
  0.0 67.0 jit_solution(17367532711759955927)
XLA Ops:
  0.0 0.0 copy-start
  0.0 33.4 %shard_map.73 = (bf16[768,512]{1,0:T(8,128)(2,1)}, f32[1,768]{1,0:T(1,128)}) custom-call(f32[4,768]{1,0:T(4,128)} %decay_ref.1, bf16[768,512]{1,0:T(8,128)(2,1)} %q_ref.1, bf16[768,512]{1,0:T(8,128)(2,1)} %k_ref.1, bf16[768,512]{1,0:T(8,128)(2,1)} %v_ref.1, bf16[768,512]{1,0:T(8,128)(2,1)} %gate_ref.1, f32[1,512]{1,0:T(1,128)} %bitcast.1), custom_call_target="tpu_custom_call" | custom-call | tf_op jit(solution)/shard_map/pallas_call | solution.py:199
  33.4 0.0 copy-done
  33.4 0.0 copy-start.1
  33.4 1.1 %copy-done.1 = bf16[768,512]{1,0:T(8,128)(2,1)S(1)} copy-done((bf16[768,512]{1,0:T(8,128)(2,1)S(1)}, bf16[768,512]{1,0:T(8,128)(2,1)}, u32[]{:S(2)}) %copy-start.1) | copy-done | bytes 786456
  34.5 0.0 copy-start.2
  34.5 0.7 %copy-done.2 = f32[1,768]{1,0:T(1,128)S(1)} copy-done((f32[1,768]{1,0:T(1,128)S(1)}, f32[1,768]{1,0:T(1,128)}, u32[]{:S(2)}) %copy-start.2) | copy-done | bytes 3096
  35.2 31.0 %shard_map.74 = bf16[768,384]{1,0:T(8,128)(2,1)S(1)} custom-call(bf16[768,512]{1,0:T(8,128)(2,1)S(1)} %copy-done.1, bf16[512,3072]{1,0:T(8,128)(2,1)S(1)} %copy-done, f32[1,768]{1,0:T(1,128)S(1)} %copy-done.2), custom_call_target="tpu_custom_call" | custom-call | tf_op jit(solution)/shard_map/pallas_call | solution.py:369
  66.2 0.8 %copy.9 = bf16[768,384]{1,0:T(8,128)(2,1)} copy(bf16[768,384]{1,0:T(8,128)(2,1)S(1)} %shard_map.74) | data formatting | bytes 1179648
Async XLA Ops:
  0.0 33.4 %copy-start = (bf16[512,3072]{1,0:T(8,128)(2,1)S(1)}, bf16[512,3072]{1,0:T(8,128)(2,1)}, u32[]{:S(2)}) copy-start(bf16[512,3072]{1,0:T(8,128)(2,1)} %w_ref.1) | copy-start | bytes 9437188
  33.4 1.1 %copy-start.1 = (bf16[768,512]{1,0:T(8,128)(2,1)S(1)}, bf16[768,512]{1,0:T(8,128)(2,1)}, u32[]{:S(2)}) copy-start(bf16[768,512]{1,0:T(8,128)(2,1)} %get-tuple-element.7.a_ref) | copy-start | bytes 2359300
  34.5 0.7 %copy-start.2 = (f32[1,768]{1,0:T(1,128)S(1)}, f32[1,768]{1,0:T(1,128)}, u32[]{:S(2)}) copy-start(f32[1,768]{1,0:T(1,128)} %get-tuple-element.8.sq_ref) | copy-start | bytes 9220

commit v6 on v5

--- a/solution.py
+++ b/solution.py
@@ -12,7 +12,7 @@
 
 def exchange_kernel(
     decay_ref, q_ref, k_ref, v_ref, gate_ref, gain_ref, o_ref, sq_ref,
-    state_ref, total_ref, first_total_ref, first_state_ref, cumulative_ref, attention, states, totals, row_state, row_total, rows_got, row_totals_got, back, mine,
+    state_ref, total_ref, first_total_ref, first_state_ref, cumulative_ref, attention, factor, scaled_q, states, totals, row_state, row_total, rows_got, row_totals_got, back, mine,
     state_send, state_recv, total_send, total_recv, row_send, row_recv,
     row_total_send, row_total_recv, back_send, back_recv,
 ):
@@ -105,6 +105,11 @@
             scores = lax.dot_general(
                 q_ref[rows, columns], k_ref[rows, columns], (((1,), (1,)), ((), ())),
                 preferred_element_type=jnp.float32,
+            )
+            gates = jax.nn.sigmoid(gate_ref[rows, columns].astype(jnp.float32))
+            factor[rows, columns] = gain_ref[:, columns] * gates
+            scaled_q[rows, columns] = q_ref[rows, columns].astype(jnp.float32) * jnp.exp(
+                by_token[rows, h : h + 1]
             )
             spread = by_token[rows, h : h + 1] - cumulative_ref[h : h + 1, rows]
             decay = jnp.where(causal, jnp.exp(jnp.where(causal, spread, 0.0)), 0.0)
@@ -174,14 +179,12 @@
             rows = slice(block * BLOCK, (block + 1) * BLOCK)
             if block == 1:
                 start = jnp.exp(first_total_ref[h : h + 1, :]) * start + first_state_ref[h]
-            query = q_ref[rows, columns].astype(jnp.float32) * jnp.exp(by_token[rows, h : h + 1])
             full = attention[rows, columns] + jnp.dot(
-                query, start, precision=lax.Precision.HIGHEST,
+                scaled_q[rows, columns], start, precision=lax.Precision.HIGHEST,
                 preferred_element_type=jnp.float32,
             )
             squares[block] = squares[block] + jnp.sum(full * full, axis=1, keepdims=True)
-            gates = jax.nn.sigmoid(gate_ref[rows, columns].astype(jnp.float32))
-            o_ref[rows, columns] = (full * gain_ref[:, columns] * gates).astype(jnp.bfloat16)
+            o_ref[rows, columns] = (full * factor[rows, columns]).astype(jnp.bfloat16)
     for block in range(2):
         spread = jnp.broadcast_to(squares[block], (BLOCK, HEAD))
         sq_ref[:, block * BLOCK : (block + 1) * BLOCK] = jnp.transpose(spread)[:1]
@@ -210,6 +213,8 @@
             pltpu.VMEM((8, HEAD), jnp.float32),
             pltpu.VMEM((columns // HEAD, HEAD, HEAD), jnp.float32),
             pltpu.VMEM((8, tokens), jnp.float32),
+            pltpu.VMEM((tokens, columns), jnp.float32),
+            pltpu.VMEM((tokens, columns), jnp.float32),
             pltpu.VMEM((tokens, columns), jnp.float32),
             block, sums,
             pltpu.VMEM((rows, HEAD), jnp.bfloat16),

time: 67.2 us -> 67 us (level)
  no operation moved by 1% of the time
where the time goes in v6:
time: 67 us; the launch traced here: 66.8 us
  Pallas kernels  64.2 us (96%)
  local copies, waits for them, and re-layouts  2.62 us (4%)
    pallas_call x1, Pallas kernels, exchange(): pl.pallas_call(exchange_kernel, out_shape=[jax.ShapeDtypeStruct((tokens,...  33.2 us
    pallas_call x1, Pallas kernels, project(): pl.pallas_call(project_kernel, out_shape=jax.ShapeDtypeStruct((tokens, wi...  31 us
    unnamed x7, local copies, waits for them, and re-layouts  2.62 us

profile of v6, /device:TPU:1, one launch (start us, length us, event | category | flops | bytes accessed | tf_op | source)
XLA Modules:
  0.0 66.8 jit_solution(12043383388716167981)
XLA Ops:
  0.0 0.0 copy-start
  0.0 33.2 %shard_map.73 = (bf16[768,512]{1,0:T(8,128)(2,1)}, f32[1,768]{1,0:T(1,128)}) custom-call(f32[4,768]{1,0:T(4,128)} %decay_ref.1, bf16[768,512]{1,0:T(8,128)(2,1)} %q_ref.1, bf16[768,512]{1,0:T(8,128)(2,1)} %k_ref.1, bf16[768,512]{1,0:T(8,128)(2,1)} %v_ref.1, bf16[768,512]{1,0:T(8,128)(2,1)} %gate_ref.1, f32[1,512]{1,0:T(1,128)} %bitcast.1), custom_call_target="tpu_custom_call" | custom-call | tf_op jit(solution)/shard_map/pallas_call | solution.py:202
  33.2 0.0 copy-done
  33.2 0.0 copy-start.1
  33.2 1.1 %copy-done.1 = bf16[768,512]{1,0:T(8,128)(2,1)S(1)} copy-done((bf16[768,512]{1,0:T(8,128)(2,1)S(1)}, bf16[768,512]{1,0:T(8,128)(2,1)}, u32[]{:S(2)}) %copy-start.1) | copy-done | bytes 786456
  34.4 0.0 copy-start.2
  34.4 0.7 %copy-done.2 = f32[1,768]{1,0:T(1,128)S(1)} copy-done((f32[1,768]{1,0:T(1,128)S(1)}, f32[1,768]{1,0:T(1,128)}, u32[]{:S(2)}) %copy-start.2) | copy-done | bytes 3096
  35.0 31.0 %shard_map.74 = bf16[768,384]{1,0:T(8,128)(2,1)S(1)} custom-call(bf16[768,512]{1,0:T(8,128)(2,1)S(1)} %copy-done.1, bf16[512,3072]{1,0:T(8,128)(2,1)S(1)} %copy-done, f32[1,768]{1,0:T(1,128)S(1)} %copy-done.2), custom_call_target="tpu_custom_call" | custom-call | tf_op jit(solution)/shard_map/pallas_call | solution.py:374
  66.0 0.8 %copy.9 = bf16[768,384]{1,0:T(8,128)(2,1)} copy(bf16[768,384]{1,0:T(8,128)(2,1)S(1)} %shard_map.74) | data formatting | bytes 1179648
Async XLA Ops:
  0.0 33.2 %copy-start = (bf16[512,3072]{1,0:T(8,128)(2,1)S(1)}, bf16[512,3072]{1,0:T(8,128)(2,1)}, u32[]{:S(2)}) copy-start(bf16[512,3072]{1,0:T(8,128)(2,1)} %w_ref.1) | copy-start | bytes 9437188
  33.2 1.1 %copy-start.1 = (bf16[768,512]{1,0:T(8,128)(2,1)S(1)}, bf16[768,512]{1,0:T(8,128)(2,1)}, u32[]{:S(2)}) copy-start(bf16[768,512]{1,0:T(8,128)(2,1)} %get-tuple-element.7.a_ref) | copy-start | bytes 2359300
  34.4 0.7 %copy-start.2 = (f32[1,768]{1,0:T(1,128)S(1)}, f32[1,768]{1,0:T(1,128)}, u32[]{:S(2)}) copy-start(f32[1,768]{1,0:T(1,128)} %get-tuple-element.8.sq_ref) | copy-start | bytes 9220
